TPU v7x, 32 devices: a whole 2x2x4 slice. The times are simulated.
32 devices in a mesh: visit: 8 (over z, y), patch: 4 (over x, core).
Axes of the slice: x: 2, y: 2, z: 4, core: 2. Of those that a mesh axis runs over, the one named last changes fastest.
Arguments:
- warped_tiles: bfloat16 [2048, 128, 128], P(('visit', 'patch')), may hold values from -12 to 12
- coefficients: bfloat16 [2048, 5], P(('visit', 'patch')), may hold values from -5 to 5
- tile_weight: bfloat16 [2048], P(('visit', 'patch')), may hold values from 0.01 to 0.15
- tile_cell: int32 [2048], P(('visit', 'patch')), may hold values from 0 to 63
- tile_valid: int32 [2048], P(('visit', 'patch')), may hold values 0 or 1
- dest_patch: int32 [2048], P(('visit', 'patch')), may hold values from 0 to 3, as said below
- basis_taps: bfloat16 [5, 2, 21], replicated, may hold values from -1.25 to 1.25
- filter_taps: bfloat16 [2, 41], replicated, may hold values from -1 to 1
Outputs:
- coadd_image: float32 [4, 1024, 1024], P('patch', 'visit')
- detection_map: float32 [4, 1024, 1024], P('patch', 'visit')
Inputs may be any that keep to these rules, and one draw needn't show every extreme that they name: `dest_patch`: the 64 tiles of one device name at most 32 tiles for any one patch; in every draw one patch receives exactly 32 tiles from every device.
All inputs are finite; a program needn't handle non-finite values. No bound on the sum of `tile_valid` on one device may be relied on, other than what follows from the above.
Results may differ from a plain program's by a relative error of at most 0.0067.
Values may be sent and summed in bfloat16 or wider, within the bound.
No kernel may reach another device: no remote copies, remote signals or barrier semaphores. Data moves between devices by JAX's collectives and lax.ppermute only.
A program may use at most 64 MiB of HBM per device.

v0:
```python
import jax
import jax.numpy as jnp
from jax import lax
from jax.sharding import PartitionSpec as P

CELL_ROWS = 8
CELL_COLS = 8


def with_halo(cells, sides, width):
    for axis, dim in sides:
        count = lax.axis_size(axis)
        ends = count - 1
        head = lax.slice_in_dim(cells, 0, width, axis=dim)
        tail = lax.slice_in_dim(cells, cells.shape[dim] - width, cells.shape[dim], axis=dim)
        cells = jnp.concatenate(
            [
                lax.ppermute(tail, axis, [(i, (i + 1) % count) for i in range(ends)]),
                cells,
                lax.ppermute(head, axis, [((i + 1) % count, i) for i in range(ends)]),
            ],
            axis=dim,
        )
    return cells


def band_matrix(taps, nrows, ncols, shift):
    row_index = lax.broadcasted_iota(jnp.int32, (nrows, ncols), 0)
    col_index = lax.broadcasted_iota(jnp.int32, (nrows, ncols), 1)
    offset_map = col_index - row_index + shift
    total = jnp.zeros((nrows, ncols), jnp.float32)
    for position in range(taps.shape[0]):
        total = total + jnp.where(offset_map == position, taps[position], jnp.float32(0.0))
    return total


def basis_mats(basis_taps, size):
    reach = (basis_taps.shape[2] - 1) // 2
    row_mats = []
    col_mats = []
    for basis in range(basis_taps.shape[0]):
        row_mats.append(band_matrix(basis_taps[basis, 0].astype(jnp.float32), size, size, reach))
        col_mats.append(band_matrix(basis_taps[basis, 1].astype(jnp.float32), size, size, reach).T)
    return (
        jnp.stack(row_mats).astype(jnp.bfloat16),
        jnp.concatenate(col_mats, axis=1).astype(jnp.bfloat16),
    )


def match_one(tile_data, scale_row, row_stack, col_joined):
    size = tile_data.shape[0]
    nbasis = row_stack.shape[0]
    columns_pass = jnp.dot(tile_data, col_joined, preferred_element_type=jnp.float32).reshape(
        size, nbasis, size
    )
    scaled = (columns_pass * scale_row.astype(jnp.float32)[None, :, None]).astype(jnp.bfloat16)
    return jnp.einsum("bik,kbj->ij", row_stack, scaled, preferred_element_type=jnp.float32).astype(
        jnp.bfloat16
    )


def shards(
    warped_tiles,
    coefficients,
    tile_weight,
    tile_cell,
    tile_valid,
    dest_patch,
    basis_taps,
    filter_taps,
):
    count = warped_tiles.shape[0]
    size = warped_tiles.shape[1]
    patches = lax.axis_size("patch")
    capacity = 2 * count // patches
    row_stack, col_joined = basis_mats(basis_taps, size)
    effective = (tile_weight.astype(jnp.float32) * tile_valid.astype(jnp.float32)).astype(
        jnp.bfloat16
    )
    scales = (coefficients.astype(jnp.float32) * effective.astype(jnp.float32)[:, None]).astype(
        jnp.bfloat16
    )
    patch_ids = jnp.arange(patches, dtype=jnp.int32)
    dest_onehot = (dest_patch[:, None] == patch_ids[None, :]).astype(jnp.int32)
    earlier = jnp.cumsum(dest_onehot, axis=0) - dest_onehot
    slot_index = jnp.sum(earlier * dest_onehot, axis=1)
    slot_ids = jnp.arange(capacity, dtype=jnp.int32)
    selector = (
        (dest_patch[None, None, :] == patch_ids[:, None, None])
        & (slot_index[None, None, :] == slot_ids[None, :, None])
    ).astype(jnp.bfloat16)

    def pack(values):
        return jnp.einsum(
            "dck,k...->dc...", selector, values, preferred_element_type=jnp.float32
        ).astype(jnp.bfloat16)

    def match_pair(item_pair):
        return match_one(item_pair[0], item_pair[1], row_stack, col_joined)

    send_weight = pack(effective)
    send_cell = pack(tile_cell.astype(jnp.bfloat16))
    tiles_part = lax.all_to_all(
        pack(warped_tiles), "patch", split_axis=0, concat_axis=0, tiled=True
    )
    scales_part = lax.all_to_all(pack(scales), "patch", split_axis=0, concat_axis=0, tiled=True)
    weight_part = lax.all_to_all(send_weight, "patch", split_axis=0, concat_axis=0, tiled=True)
    cell_part = lax.all_to_all(send_cell, "patch", split_axis=0, concat_axis=0, tiled=True)
    shape = tiles_part.shape
    flat_tiles = tiles_part.reshape((shape[0] * shape[1],) + shape[2:])
    flat_scales = scales_part.reshape(shape[0] * shape[1], scales_part.shape[2])
    matched_flat = lax.map(match_pair, (flat_tiles, flat_scales))
    received = matched_flat.reshape(shape)
    slots = received.shape[0] * received.shape[1]
    flat_matched = received.reshape(slots, size, size)
    cell_ids = cell_part.reshape(slots).astype(jnp.int32)
    cell_onehot = (
        (cell_ids[:, None] == jnp.arange(CELL_ROWS * CELL_COLS, dtype=jnp.int32)[None, :])
        .reshape(slots, CELL_ROWS, CELL_COLS)
        .astype(jnp.bfloat16)
    )
    image = jnp.einsum(
        "sgh,sij->gihj", cell_onehot, flat_matched, preferred_element_type=jnp.float32
    ).reshape(CELL_ROWS * size, CELL_COLS * size)
    weight_sums = jnp.einsum(
        "sgh,s->gh", cell_onehot, weight_part.reshape(slots), preferred_element_type=jnp.float32
    )
    weight_rows = jnp.repeat(weight_sums, size, axis=0)
    reach = (filter_taps.shape[1] - 1) // 2
    width = CELL_COLS * size
    numer, denom = (
        lax.psum_scatter(image, "visit", scatter_dimension=0, tiled=True),
        lax.psum_scatter(weight_rows, "visit", scatter_dimension=0, tiled=True),
    )
    coadd_strip = numer / (jnp.repeat(denom, size, axis=1) + 1.0)
    extended = with_halo(coadd_strip.astype(jnp.bfloat16), (("visit", 0),), reach)
    strip_rows = coadd_strip.shape[0]
    vertical_mat = band_matrix(filter_taps[0], strip_rows, strip_rows + 2 * reach, 0).astype(
        jnp.bfloat16
    )
    vertical = jnp.dot(vertical_mat, extended, preferred_element_type=jnp.float32).astype(
        jnp.bfloat16
    )
    horizontal_mat = band_matrix(filter_taps[1], width, width, reach).T.astype(jnp.bfloat16)
    filtered = jnp.dot(vertical, horizontal_mat, preferred_element_type=jnp.float32)
    return (coadd_strip[None], filtered[None])


def solution(mesh):
    in_specs = (
        P(("visit", "patch"), None, None),
        P(("visit", "patch"), None),
        P(("visit", "patch")),
        P(("visit", "patch")),
        P(("visit", "patch")),
        P(("visit", "patch")),
        P(),
        P(),
    )
    out_specs = (P("patch", "visit", None), P("patch", "visit", None))
    return jax.shard_map(shards, mesh=mesh, in_specs=in_specs, out_specs=out_specs, check_vma=False)
```

profile of v0, /device:TPU:8, one launch (start us, length us, event | category | flops | bytes accessed | tf_op | source)
XLA Modules:
  0.0 600.7 jit_solution(17736880912305134509)
XLA Ops:
  10.9 3.2 all-to-all-start.2
  15.7 5.6 convolution_convert_fusion
  22.6 3.3 all-to-all-start.3
  25.9 3.8 all-to-all-done.3
  29.6 3.2 all-to-all-start.1
  33.5 3.2 all-to-all-done.1
  36.7 4.9 all-to-all-start
  45.0 13.1 %fusion.326 = bf16[5,128,128]{2,1,0:T(8,128)(2,1)S(1)} fusion(f32[]{:T(128)} %bitcast.139, f32[]{:T(128)} %bitcast.138, f32[]{:T(128)} %bitcast.137, f32[]{:T(128)} %bitcast.136, f32[]{:T(128)} %bitcast.135, f32[]{:T(128)} %bitcast.134, f32[]{:T(128)} %bitcast.133, f32[]{:T(128)} %bitcast.132, f32[]{:T(128)} %bitcast.131, f32[]{:T(128)} %bitcast.130, ...), kind=kLoop, calls=%fused_computation.262 | loop fusion | flops 1064959 | bytes 32852
  58.8 13.1 %fusion.331 = bf16[128,640]{0,1:T(8,128)(2,1)S(1)} fusion(f32[]{:T(128)} %bitcast.32, f32[]{:T(128)} %bitcast.31, f32[]{:T(128)} %bitcast.30, f32[]{:T(128)} %bitcast.29, f32[]{:T(128)} %bitcast.28, f32[]{:T(128)} %bitcast.27, f32[]{:T(128)} %bitcast.26, f32[]{:T(128)} %bitcast.25, f32[]{:T(128)} %bitcast.24, f32[]{:T(128)} %bitcast.23, f32[]{:T(128)} %bitcast.22, ...), kind=kLoop, calls=%fused_computation.267 | loop fusion | flops 1064959 | bytes 32852
  72.7 13.2 %fusion.327 = bf16[5,128,128]{2,1,0:T(8,128)(2,1)S(1)} fusion(bf16[5,128,128]{2,1,0:T(8,128)(2,1)S(1)} %fusion.326, f32[]{:T(128)} %bitcast.160, f32[]{:T(128)} %bitcast.159, f32[]{:T(128)} %bitcast.158, f32[]{:T(128)} %bitcast.157, f32[]{:T(128)} %bitcast.156, f32[]{:T(128)} %bitcast.155, f32[]{:T(128)} %bitcast.154, f32[]{:T(128)} %bitcast.153, ...), kind=kLoop, calls=%fused_computation.263 | loop fusion | flops 1064960 | bytes 32852
  86.6 13.3 %fusion.328 = bf16[5,128,128]{2,1,0:T(8,128)(2,1)S(1)} fusion(bf16[5,128,128]{2,1,0:T(8,128)(2,1)S(1)} %fusion.327, f32[]{:T(128)} %bitcast.181, f32[]{:T(128)} %bitcast.180, f32[]{:T(128)} %bitcast.179, f32[]{:T(128)} %bitcast.178, f32[]{:T(128)} %bitcast.177, f32[]{:T(128)} %bitcast.176, f32[]{:T(128)} %bitcast.175, f32[]{:T(128)} %bitcast.174, ...), kind=kLoop, calls=%fused_computation.264 | loop fusion | flops 1064960 | bytes 32852
  100.6 13.3 %fusion.329 = bf16[5,128,128]{2,1,0:T(8,128)(2,1)S(1)} fusion(bf16[5,128,128]{2,1,0:T(8,128)(2,1)S(1)} %fusion.328, f32[]{:T(128)} %bitcast.202, f32[]{:T(128)} %bitcast.201, f32[]{:T(128)} %bitcast.200, f32[]{:T(128)} %bitcast.199, f32[]{:T(128)} %bitcast.198, f32[]{:T(128)} %bitcast.197, f32[]{:T(128)} %bitcast.196, f32[]{:T(128)} %bitcast.195, ...), kind=kLoop, calls=%fused_computation.265 | loop fusion | flops 1064960 | bytes 32852
  114.5 13.4 %fusion.330 = bf16[5,128,128]{2,1,0:T(8,128)(2,1)S(1)} fusion(bf16[5,128,128]{2,1,0:T(8,128)(2,1)S(1)} %fusion.329, f32[]{:T(128)} %bitcast.223, f32[]{:T(128)} %bitcast.222, f32[]{:T(128)} %bitcast.221, f32[]{:T(128)} %bitcast.220, f32[]{:T(128)} %bitcast.219, f32[]{:T(128)} %bitcast.218, f32[]{:T(128)} %bitcast.217, f32[]{:T(128)} %bitcast.216, ...), kind=kLoop, calls=%fused_computation.266 | loop fusion | flops 1064960 | bytes 32852 | tf_op jit(solution)/shard_map/stack | solution.py:45
  128.7 13.3 %fusion.332 = bf16[128,640]{0,1:T(8,128)(2,1)S(1)} fusion(bf16[128,640]{0,1:T(8,128)(2,1)S(1)} %fusion.331, f32[]{:T(128)} %bitcast.53, f32[]{:T(128)} %bitcast.52, f32[]{:T(128)} %bitcast.51, f32[]{:T(128)} %bitcast.50, f32[]{:T(128)} %bitcast.49, f32[]{:T(128)} %bitcast.48, f32[]{:T(128)} %bitcast.47, f32[]{:T(128)} %bitcast.46, f32[]{:T(128)} %bitcast.45, ...), kind=kLoop, calls=%fused_computation.268 | loop fusion | flops 1064960 | bytes 32852
  142.7 13.2 %fusion.333 = bf16[128,640]{0,1:T(8,128)(2,1)S(1)} fusion(bf16[128,640]{0,1:T(8,128)(2,1)S(1)} %fusion.332, f32[]{:T(128)} %bitcast.74, f32[]{:T(128)} %bitcast.73, f32[]{:T(128)} %bitcast.72, f32[]{:T(128)} %bitcast.71, f32[]{:T(128)} %bitcast.70, f32[]{:T(128)} %bitcast.69, f32[]{:T(128)} %bitcast.68, f32[]{:T(128)} %bitcast.67, f32[]{:T(128)} %bitcast.66, ...), kind=kLoop, calls=%fused_computation.269 | loop fusion | flops 1064960 | bytes 32852
  156.6 13.2 %fusion.334 = bf16[128,640]{0,1:T(8,128)(2,1)S(1)} fusion(bf16[128,640]{0,1:T(8,128)(2,1)S(1)} %fusion.333, f32[]{:T(128)} %bitcast.95, f32[]{:T(128)} %bitcast.94, f32[]{:T(128)} %bitcast.93, f32[]{:T(128)} %bitcast.92, f32[]{:T(128)} %bitcast.91, f32[]{:T(128)} %bitcast.90, f32[]{:T(128)} %bitcast.89, f32[]{:T(128)} %bitcast.88, f32[]{:T(128)} %bitcast.87, ...), kind=kLoop, calls=%fused_computation.270 | loop fusion | flops 1064960 | bytes 32852
  170.6 13.1 %fusion.335 = bf16[128,640]{0,1:T(8,128)(2,1)S(1)} fusion(bf16[128,640]{0,1:T(8,128)(2,1)S(1)} %fusion.334, f32[]{:T(128)} %bitcast.116, f32[]{:T(128)} %bitcast.115, f32[]{:T(128)} %bitcast.114, f32[]{:T(128)} %bitcast.113, f32[]{:T(128)} %bitcast.112, f32[]{:T(128)} %bitcast.111, f32[]{:T(128)} %bitcast.110, f32[]{:T(128)} %bitcast.109, f32[]{:T(128)} %bitcast.108, ...), kind=kLoop, calls=%fused_computation.271 | loop fusion | flops 1064960 | bytes 32852 | tf_op jit(solution)/shard_map/concatenate | solution.py:46
  185.2 5.8 copy.29
  191.1 233.4 %while.10 = (s32[]{:T(128)}, bf16[128,128,128]{1,2,0:T(8,128)(2,1)}, bf16[128,128,128]{2,1,0:T(8,128)(2,1)}, bf16[128,640]{0,1:T(8,128)(2,1)S(1)}, bf16[128,5]{1...) while((s32[]{:T(128)}, bf16[128,128,128]{1,2,0:T(8,128)(2,1)}, ...), condition=%wide.region_3.4_spmd, body=%wide.region_2.3_spmd.sunk | while | flops 42123272 | bytes 394371 | solution.py:112
  196.5 1.8 fusion.479
  198.4 1.8 fusion.479
  202.0 1.8 fusion.479
  205.7 1.8 fusion.479
  216.6 1.8 fusion.479
  218.4 1.8 fusion.479
  222.1 1.8 fusion.479
  223.9 1.8 fusion.479
  227.6 1.8 fusion.479
  229.4 1.8 fusion.479
  231.2 1.8 fusion.479
  234.9 1.8 fusion.479
  238.5 1.8 fusion.479
  245.8 1.8 fusion.479
  249.5 1.8 fusion.479
  253.1 1.8 fusion.479
  260.4 1.8 fusion.479
  267.7 1.8 fusion.479
  275.0 1.8 fusion.479
  282.3 1.8 fusion.479
  285.9 1.8 fusion.479
  293.2 1.8 fusion.479
  296.9 1.8 fusion.479
  300.5 1.8 fusion.479
  307.8 1.8 fusion.479
  311.5 1.8 fusion.479
  318.8 1.8 fusion.479
  324.2 1.8 fusion.479
  337.0 1.8 fusion.479
  358.9 1.8 fusion.479
  362.5 1.8 fusion.479
  369.8 1.8 fusion.479
  380.7 1.8 fusion.479
  384.4 1.8 fusion.479
  391.7 1.8 fusion.479
  402.6 1.8 fusion.479
  413.6 1.8 fusion.479
  424.5 6.7 %copy.39 = bf16[128,128,128,1]{2,0,3,1:T(8,128)(2,1)} copy(bf16[128,128,128,1]{1,2,0,3:T(8,128)(2,1)} %bitcast.475) | data formatting | bytes 8388608 | tf_op jit(solution)/shard_map/while | solution.py:112
  431.2 2.9 convolution_bitcast_fusion
  434.4 2.9 copy.58
  441.7 85.9 %reduce-scatter.3.cloned.1.call-done = f32[128,1024]{1,0:T(8,128)} async-done(((f32[1024,1024]{1,0:T(8,128)}), f32[128,1024]{1,0:T(8,128)}) %reduce-scatter.3.cloned.1.call-update) | async-done | bytes 524304 | tf_op jit(solution)/shard_map/reduce_scatter | solution.py:132
  527.8 2.0 fusion.438
  529.8 3.4 collective-permute-start
  533.2 3.5 collective-permute-start.1
  589.0 4.8 fusion.59
  (281 shorter events, 190.1 us)
Async XLA Ops:
  7.2 14.1 %copy-start.2 = (bf16[64,5]{0,1:T(8,128)(2,1)S(1)}, bf16[64,5]{0,1:T(8,128)(2,1)}, u32[]{:S(2)}) copy-start(bf16[64,5]{0,1:T(8,128)(2,1)} %param.11) | copy-start | bytes 1924
  7.2 18.7 %copy-start.1 = (bf16[5,2,21]{2,1,0:T(2,128)(2,1)S(1)}, bf16[5,2,21]{2,1,0:T(2,128)(2,1)}, u32[]{:S(2)}) copy-start(bf16[5,2,21]{2,1,0:T(2,128)(2,1)} %param.16) | copy-start | bytes 1264
  10.9 11.7 %all-to-all-start.2 = ((bf16[4,1,32]{2,1,0:T(2,128)(2,1)}), bf16[4,1,32]{2,1,0:T(2,128)(2,1)S(1)}, u32[]{:S(2)}, u32[]{:S(2)}) async-start(bf16[4,1,32]{2,1,0:T(2,128)(2,1)} %copy.32), calls=%async_computation.2 | async-start | bytes 4096 | tf_op jit(solution)/shard_map/all_to_all | solution.py:108
  22.6 7.0 %all-to-all-start.3 = ((bf16[4,1,32]{2,1,0:T(2,128)(2,1)}), bf16[4,1,32]{2,1,0:T(2,128)(2,1)S(1)}, u32[]{:S(2)}, u32[]{:S(2)}) async-start(bf16[4,1,32]{2,1,0:T(2,128)(2,1)} %copy.35), calls=%async_computation.4 | async-start | bytes 4096 | tf_op jit(solution)/shard_map/all_to_all | solution.py:107
  29.6 7.0 %all-to-all-start.1 = ((bf16[4,32,5]{1,2,0:T(8,128)(2,1)}), bf16[4,32,5]{1,2,0:T(8,128)(2,1)S(1)}, u32[]{:S(2)}, u32[]{:S(2)}) async-start(bf16[4,32,5]{1,2,0:T(8,128)(2,1)} %convolution_convert_fusion.2), calls=%async_computation.1 | async-start | bytes 16384 | tf_op jit(solution)/shard_map/all_to_all | solution.py:106
  36.7 148.6 %all-to-all-start = ((bf16[4,32,128,128]{3,1,2,0:T(8,128)(2,1)}), bf16[4,32,128,128]{3,1,2,0:T(8,128)(2,1)}, u32[]{:S(2)}, u32[]{:S(2)}) async-start(bf16[4,32,128,128]{3,1,2,0:T(8,128)(2,1)} %convolution_convert_fusion), calls=%async_computation | async-start | bytes 8388608 | tf_op jit(solution)/shard_map/all_to_all | solution.py:103
  41.6 399.2 %reduce-scatter.5.cloned.1.call-start = ((), (), s32[]{:S(2)}) async-start(), calls=%async_computation.7 | async-start | bytes 589824 | tf_op jit(solution)/shard_map/reduce_scatter | solution.py:133
  185.1 342.5 %reduce-scatter.3.cloned.1.call-start = ((), (), s32[]{:S(2)}) async-start(), calls=%async_computation.6 | async-start | bytes 4718592 | tf_op jit(solution)/shard_map/reduce_scatter | solution.py:132
  437.3 0.7 copy-start
  529.8 59.2 %collective-permute-start = (bf16[20,1024]{1,0:T(8,128)(2,1)S(1)}, bf16[20,1024]{1,0:T(8,128)(2,1)S(1)}, u32[]{:S(2)}, u32[]{:S(2)}) collective-permute-start(bf16[20,1024]{1,0:T(8,128)(2,1)S(1)} %get-tuple-element.67), channel_id=1, source_target_pairs={{0,4},{4,8},{8,12},{12,16},{16,20},{20,24},{24,28},{1,5},{5,9},{9,... | collective-permute-start | bytes 122888 | tf_op jit(solution)/shard_map/ppermute | solution.py:18
  533.2 55.8 %collective-permute-start.1 = (bf16[20,1024]{1,0:T(8,128)(2,1)S(1)}, bf16[20,1024]{1,0:T(8,128)(2,1)S(1)}, u32[]{:S(2)}, u32[]{:S(2)}) collective-permute-start(bf16[20,1024]{1,0:T(8,128)(2,1)S(1)} %get-tuple-element.68), channel_id=1, source_target_pairs={{4,0},{8,4},{12,8},{16,12},{20,16},{24,20},{28,24},{5,1},{9,5},{13... | collective-permute-start | bytes 122888 | tf_op jit(solution)/shard_map/ppermute | solution.py:20
Sparse Core Ops, SparseCore 0:
  185.2 64.0 reduce-scatter.4
  437.5 90.0 reduce-scatter.2
where the time goes:
time: 613 us; the launch traced here: 601 us
  matrix products  248 us (40%)
  other arithmetic  139 us (23%)
  waiting for transfers between devices  92.9 us (15%)
  between operations  65.8 us (11%)
  local copies, waits for them, and re-layouts  32.9 us (5%)
  starting transfers between devices  21.7 us (4%)
    dot_general x128, matrix products, match_one(): jnp.einsum('bik,kbj->ij', row_stack, scaled, preferred_element_type=jnp.f...  232 us
    unnamed x8, other arithmetic  106 us
    reduce_scatter x1, waiting for transfers between devices, shards(): lax.psum_scatter(image, 'visit', scatter_dimension=0, tiled=True)  85.9 us
    slice x20, local copies, waits for them, and re-layouts, band_matrix(): taps[position]  14 us
    another operation x1, other arithmetic, basis_mats(): jnp.stack(row_mats).astype(jnp.bfloat16)  13.4 us
    concatenate x1, other arithmetic, basis_mats(): jnp.concatenate(col_mats, axis=1).astype(jnp.bfloat16)  13.1 us
  transfers between devices with their start and end apart: 8, of which 3 were waited for; matrix products, arithmetic and copies ran while one was open for 68% of the time, Pallas kernels for 0%

commit v1 on v0

v1 whole, which is shorter than its diff:
```python
import functools

import jax
import jax.numpy as jnp
from jax import lax
from jax.experimental import pallas as pl
from jax.experimental.pallas import tpu as pltpu
from jax.sharding import PartitionSpec as P

CELL_ROWS = 8
CELL_COLS = 8
CELLS = CELL_ROWS * CELL_COLS
SETS = (((0, 2), (2, 4)), ((4, 6), (6, 8)))
UNROLL = 4
EDGE = 32
WROWS = 16
F32 = jnp.float32
BF16 = jnp.bfloat16


def in_vmem():
    return pl.BlockSpec(memory_space=pltpu.VMEM)


def in_smem():
    return pl.BlockSpec(memory_space=pltpu.SMEM)


def rows_shape(rows, dtype=BF16):
    return jax.ShapeDtypeStruct((rows, 128), dtype)


def band(get_tap, ntaps, nrows, ncols, shift, sign):
    row = lax.broadcasted_iota(jnp.int32, (nrows, ncols), 0)
    col = lax.broadcasted_iota(jnp.int32, (nrows, ncols), 1)
    offset = sign * (col - row) + shift
    out = jnp.zeros((nrows, ncols), F32)
    for k in range(ntaps):
        out = jnp.where(offset == k, get_tap(k), out)
    return out.astype(BF16)


def basis_kernel(taps, row_out, col_out, *, nb, nt, size):
    reach = (nt - 1) // 2
    for b in range(nb):
        row_out[b * size : (b + 1) * size, :] = band(
            lambda k: taps[(b * 2) * nt + k], nt, size, size, reach, 1
        )
        col_out[b * size : (b + 1) * size, :] = band(
            lambda k: taps[(b * 2 + 1) * nt + k], nt, size, size, reach, -1
        )


def filter_mats_kernel(taps, vert_out, horiz_out, *, nt, strip, pad):
    reach = (nt - 1) // 2
    vert_out[...] = band(lambda k: taps[k], nt, strip, strip + 2 * EDGE, reach - EDGE, 1)
    horiz_out[...] = band(lambda k: taps[nt + k], nt, pad * 2 + 128, 128, reach - pad, -1)


def split3(w):
    hi = w.astype(BF16)
    rest = w - hi.astype(F32)
    mid = rest.astype(BF16)
    lo = (rest - mid.astype(F32)).astype(BF16)
    return hi, mid, lo


def store_weights(ref, base, w):
    hi, mid, lo = (part.astype(F32) for part in split3(w))
    row = lax.broadcasted_iota(jnp.int32, (WROWS, 128), 0)
    block = jnp.where(row == 0, hi, jnp.where(row == 1, mid, jnp.where(row == 2, lo, 0.0)))
    ref[base : base + WROWS, :] = block.astype(BF16)


def load_weights(ref, base):
    block = ref[base : base + WROWS, :].astype(F32)
    return jnp.sum(block, axis=0, keepdims=True)


def match_kernel(
    scal,
    keys_own,
    keys_other,
    info_own,
    info_other,
    tiles_own,
    tiles_other,
    row_cat,
    col_cat,
    *refs,
    cfg,
    cols_a,
    cols_b,
):
    X, Y, Z, V, R, nb, count = cfg
    na, nbc = cols_a[1] - cols_a[0], cols_b[1] - cols_b[0]
    h0, h1 = cols_a[0], cols_b[1]
    a_out = refs[:X]
    b_out = refs[X : X + Y]
    acc, wacc, listing, tiles, sems = refs[X + Y :]
    size = tiles.shape[1]
    parts = size // R
    x, core, y = scal[0], scal[1], scal[3]
    copies = [
        pltpu.make_async_copy(tiles_own, tiles.at[pl.ds(0, count)], sems.at[0]),
        pltpu.make_async_copy(tiles_other, tiles.at[pl.ds(count, count)], sems.at[1]),
    ]
    for copy in copies:
        copy.start()
    acc[...] = jnp.zeros_like(acc)
    wacc[...] = jnp.zeros_like(wacc)

    def lister(keys, base):
        def body(t, n):
            key = keys[t]
            h = key & (CELL_COLS - 1)
            mine = (((key >> 6) & 1) == core) & (h >= h0) & (h < h1)
            listing[n] = base + t
            return n + mine.astype(jnp.int32)

        return body

    n = lax.fori_loop(0, count, lister(keys_own, 0), jnp.int32(0))
    n = lax.fori_loop(0, count, lister(keys_other, count), n)
    for q in range(UNROLL):
        listing[n + q] = 0
    for copy in copies:
        copy.wait()
    lane = lax.broadcasted_iota(jnp.int32, (1, 128), 1)

    def step(i, carry):
        todo = []
        for q in range(UNROLL):
            k = i * UNROLL + q
            live = k < n
            t = listing[k]
            own = t < count
            t_in = jnp.where(own, t, t - count)
            key = jnp.where(own, keys_own[t_in], keys_other[t_in])
            key = jnp.where(live, key, h0)
            values = [
                jnp.where(
                    live,
                    jnp.where(own, info_own[t_in * 8 + b], info_other[t_in * 8 + b]),
                    jnp.float32(0.0),
                )
                for b in range(nb + 1)
            ]
            todo.append((t, key, values))
        for q in range(0, UNROLL, 2):
            pair = todo[q : q + 2]
            wide = jnp.concatenate([tiles[t] for t, _, _ in pair], axis=1)
            rows = jnp.dot(row_cat[...], wide, preferred_element_type=F32)
            stacked = jnp.concatenate(
                [
                    jnp.concatenate(
                        [
                            (
                                rows[b * size : (b + 1) * size, j * size : (j + 1) * size]
                                * values[b]
                            ).astype(BF16)
                            for b in range(nb)
                        ],
                        axis=1,
                    )
                    for j, (_, _, values) in enumerate(pair)
                ],
                axis=0,
            )
            out = jnp.dot(stacked, col_cat[...], preferred_element_type=F32)
            for j, (_, key, values) in enumerate(pair):
                cell = key & (CELLS - 1)
                xp = key >> 7
                g = cell >> 3
                hh = (cell & (CELL_COLS - 1)) - h0
                for part in range(parts):
                    base = j * size + part * R
                    spot = acc.at[xp, g * parts + part, hh]
                    spot[...] = spot[...] + out[base : base + R]
                wrow = wacc.at[pl.ds(xp, 1), :]
                wrow[...] = wrow[...] + jnp.where(lane == cell, values[nb], 0.0)
        return carry

    lax.fori_loop(0, (n + UNROLL - 1) // UNROLL, step, jnp.int32(0))

    for j in range(X):
        xp = lax.rem(x + j, X)

        def put_a(v, carry, j=j, xp=xp):
            for hh in range(na):
                start = pl.multiple_of((v * na + hh) * R, 16)
                a_out[j][pl.ds(start, R), :] = acc[xp, v, hh].astype(BF16)
            return carry

        lax.fori_loop(0, V, put_a, jnp.int32(0))
        store_weights(a_out[j], V * na * R, wacc[pl.ds(xp, 1), :])
    for i in range(Y):
        yp = lax.rem(y + i, Y)
        for j in range(X):
            xp = lax.rem(x + j, X)

            def put_b(z, carry, i=i, j=j, xp=xp, yp=yp):
                for hh in range(nbc):
                    start = pl.multiple_of(((j * Z + z) * nbc + hh) * R, 16)
                    b_out[i][pl.ds(start, R), :] = acc[xp, z * Y + yp, na + hh].astype(BF16)
                return carry

            lax.fori_loop(0, Z, put_b, jnp.int32(0))


def first_add_kernel(scal, *refs, cfg, na, nbc):
    X, Y, Z, V, R, _, _ = cfg
    a_in = refs[:X]
    b_in = refs[X : X + Y]
    a_out = refs[X + Y : X + 2 * Y]
    b_out = refs[X + 2 * Y :]
    y = scal[3]
    w = sum(load_weights(ref, V * na * R) for ref in a_in)
    span = na * R
    for i in range(Y):
        yp = lax.rem(y + i, Y)
        for z in range(Z):
            start = pl.multiple_of((z * Y + yp) * span, 16)
            total = sum(ref[pl.ds(start, span), :].astype(F32) for ref in a_in)
            a_out[i][z * span : (z + 1) * span, :] = total.astype(BF16)
        store_weights(a_out[i], Z * span, w)
    block = Z * nbc * R
    for j in range(X):
        total = sum(ref[j * block : (j + 1) * block, :].astype(F32) for ref in b_in)
        b_out[j][...] = total.astype(BF16)


def second_add_kernel(scal, *refs, cfg, na, nbc):
    X, Y, Z, V, R, _, _ = cfg
    a_in = refs[:Y]
    b_in = refs[Y : Y + X]
    outs = refs[Y + X :]
    z = scal[2]
    w = sum(load_weights(ref, Z * na * R) for ref in a_in)
    for k in range(Z):
        zp = lax.rem(z + k, Z)
        start = pl.multiple_of(zp * (na * R), 16)
        total = sum(ref[pl.ds(start, na * R), :].astype(F32) for ref in a_in)
        outs[k][: na * R, :] = total.astype(BF16)
        start = pl.multiple_of(zp * (nbc * R), 16)
        total = sum(ref[pl.ds(start, nbc * R), :].astype(F32) for ref in b_in)
        outs[k][na * R : (na + nbc) * R, :] = total.astype(BF16)
        store_weights(outs[k], (na + nbc) * R, w)


def coadd_kernel(scal, *refs, cfg, h0, nh):
    X, Y, Z, V, R, _, _ = cfg
    ins = refs[:Z]
    out, top, bottom = refs[Z:]
    g = (scal[2] * Y + scal[3]) // (V // CELL_ROWS)
    w = sum(load_weights(ref, nh * R) for ref in ins)
    lane = lax.broadcasted_iota(jnp.int32, (1, 128), 1)
    for hh in range(nh):
        total = sum(ref[hh * R : (hh + 1) * R, :].astype(F32) for ref in ins)
        here = jnp.where(lane == g * CELL_COLS + h0 + hh, w, 0.0)
        denom = jnp.sum(here, axis=1, keepdims=True) + 1.0
        value = total / denom
        cols = slice(hh * 128, (hh + 1) * 128)
        out[:, cols] = value
        top[:, cols] = value[:EDGE].astype(BF16)
        bottom[:, cols] = value[R - EDGE :].astype(BF16)


def detect_kernel(vert, horiz, *refs, nsets, R):
    strips = refs[:nsets]
    aboves = refs[nsets : 2 * nsets]
    belows = refs[2 * nsets : 3 * nsets]
    coadd, detect = refs[3 * nsets : 3 * nsets + 2]
    filtered = refs[3 * nsets + 2]
    base = 0
    for strip, above, below in zip(strips, aboves, belows):
        width = strip.shape[1]
        coadd[:, base : base + width] = strip[...]
        extended = jnp.concatenate([above[...], strip[...].astype(BF16), below[...]], axis=0)
        filtered[:, base : base + width] = jnp.dot(
            vert[...], extended, preferred_element_type=F32
        ).astype(BF16)
        base += width
    blocks = base // 128
    for j in range(blocks):
        lo, hi = max(j - 1, 0), min(j + 2, blocks)
        detect[:, j * 128 : (j + 1) * 128] = jnp.dot(
            filtered[:, lo * 128 : hi * 128],
            horiz[(lo - j + 1) * 128 : (hi - j + 1) * 128, :],
            preferred_element_type=F32,
        )


def shards(
    warped_tiles,
    coefficients,
    tile_weight,
    tile_cell,
    tile_valid,
    dest_patch,
    basis_taps,
    filter_taps,
):
    count, size = warped_tiles.shape[:2]
    nb, _, nt = basis_taps.shape
    nf = filter_taps.shape[1]
    patches, V = lax.axis_size("patch"), lax.axis_size("visit")
    X, Y, Z = patches // 2, 2, V // 2
    R = CELL_ROWS * size // V
    cfg = (X, Y, Z, V, R, nb, count)
    patch, visit = lax.axis_index("patch"), lax.axis_index("visit")
    scal = jnp.stack([patch // 2, patch % 2, visit // 2, visit % 2]).astype(jnp.int32)

    def send(value, move):
        pairs = []
        for v in range(V):
            for p in range(patches):
                z, y, x, core = move(v // Y, v % Y, p // 2, p % 2)
                pairs.append((v * patches + p, (z * Y + y) * patches + x * 2 + core))
        return lax.ppermute(value, ("visit", "patch"), pairs)

    def to_core(value):
        return send(value, lambda z, y, x, core: (z, y, x, 1 - core))

    def to_x(value, k):
        return send(value, lambda z, y, x, core: (z, y, (x + k) % X, core))

    def to_y(value, k):
        return send(value, lambda z, y, x, core: (z, (y + k) % Y, x, core))

    def to_z(value, k):
        return send(value, lambda z, y, x, core: ((z + k) % Z, y, x, core))

    effective = lax.reduce_precision(
        tile_weight.astype(F32) * tile_valid.astype(F32), exponent_bits=8, mantissa_bits=7
    )
    scales = lax.reduce_precision(
        coefficients.astype(F32) * effective[:, None], exponent_bits=8, mantissa_bits=7
    )
    info = jnp.concatenate(
        [scales, effective[:, None], jnp.zeros((count, 7 - nb), F32)], axis=1
    ).reshape(count * 8)
    keys = dest_patch * CELLS + tile_cell
    tiles_other = to_core(warped_tiles)
    info_other = to_core(info)
    keys_other = to_core(keys)

    row_cat, col_cat = pl.pallas_call(
        functools.partial(basis_kernel, nb=nb, nt=nt, size=size),
        out_shape=(rows_shape(nb * size), rows_shape(nb * size)),
        in_specs=[in_smem()],
        out_specs=(in_vmem(), in_vmem()),
    )(basis_taps.astype(F32).reshape(-1))
    vert, horiz = pl.pallas_call(
        functools.partial(filter_mats_kernel, nt=nf, strip=R, pad=128),
        out_shape=(
            jax.ShapeDtypeStruct((R, R + 2 * EDGE), BF16),
            rows_shape(384),
        ),
        in_specs=[in_smem()],
        out_specs=(in_vmem(), in_vmem()),
    )(filter_taps.astype(F32).reshape(-1))

    strips, tops, bottoms = [], [], []
    for cols_a, cols_b in SETS:
        na, nbc = cols_a[1] - cols_a[0], cols_b[1] - cols_b[0]
        nh = na + nbc
        outs = pl.pallas_call(
            functools.partial(match_kernel, cfg=cfg, cols_a=cols_a, cols_b=cols_b),
            out_shape=tuple(
                [rows_shape(V * na * R + WROWS)] * X + [rows_shape(X * Z * nbc * R)] * Y
            ),
            in_specs=[in_smem()] * 5
            + [pl.BlockSpec(memory_space=pl.ANY)] * 2
            + [in_vmem()] * 2,
            out_specs=tuple([in_vmem()] * (X + Y)),
            scratch_shapes=[
                pltpu.VMEM((X, V, nh, R, 128), F32),
                pltpu.VMEM((max(X, 8), 128), F32),
                pltpu.SMEM((2 * count + UNROLL,), jnp.int32),
                pltpu.VMEM((2 * count, size, size), BF16),
                pltpu.SemaphoreType.DMA((2,)),
            ],
        )(
            scal,
            keys,
            keys_other,
            info,
            info_other,
            warped_tiles,
            tiles_other,
            row_cat,
            col_cat,
        )
        a, b = outs[:X], outs[X:]
        a = [a[0]] + [to_x(a[k], k) for k in range(1, X)]
        b = [b[0]] + [to_y(b[k], k) for k in range(1, Y)]
        outs = pl.pallas_call(
            functools.partial(first_add_kernel, cfg=cfg, na=na, nbc=nbc),
            out_shape=tuple(
                [rows_shape(Z * na * R + WROWS)] * Y + [rows_shape(Z * nbc * R)] * X
            ),
            in_specs=[in_smem()] + [in_vmem()] * (X + Y),
            out_specs=tuple([in_vmem()] * (X + Y)),
        )(scal, *a, *b)
        a, b = outs[:Y], outs[Y:]
        a = [a[0]] + [to_y(a[k], k) for k in range(1, Y)]
        b = [b[0]] + [to_x(b[k], k) for k in range(1, X)]
        outs = pl.pallas_call(
            functools.partial(second_add_kernel, cfg=cfg, na=na, nbc=nbc),
            out_shape=tuple([rows_shape(nh * R + WROWS)] * Z),
            in_specs=[in_smem()] + [in_vmem()] * (X + Y),
            out_specs=tuple([in_vmem()] * Z),
        )(scal, *a, *b)
        outs = [outs[0]] + [to_z(outs[k], k) for k in range(1, Z)]
        strip, top, bottom = pl.pallas_call(
            functools.partial(coadd_kernel, cfg=cfg, h0=cols_a[0], nh=nh),
            out_shape=(
                jax.ShapeDtypeStruct((R, nh * 128), F32),
                jax.ShapeDtypeStruct((EDGE, nh * 128), BF16),
                jax.ShapeDtypeStruct((EDGE, nh * 128), BF16),
            ),
            in_specs=[in_smem()] + [in_vmem()] * Z,
            out_specs=(in_vmem(), in_vmem(), in_vmem()),
        )(scal, *outs)
        strips.append(strip)
        tops.append(top)
        bottoms.append(bottom)
    aboves = [lax.ppermute(v, "visit", [(i, i + 1) for i in range(V - 1)]) for v in bottoms]
    belows = [lax.ppermute(v, "visit", [(i + 1, i) for i in range(V - 1)]) for v in tops]
    nsets = len(SETS)
    coadd, detect = pl.pallas_call(
        functools.partial(detect_kernel, nsets=nsets, R=R),
        out_shape=(
            jax.ShapeDtypeStruct((R, CELL_COLS * size), F32),
            jax.ShapeDtypeStruct((R, CELL_COLS * size), F32),
        ),
        in_specs=[in_vmem()] * (2 + 3 * nsets),
        out_specs=(in_vmem(), in_vmem()),
        scratch_shapes=[pltpu.VMEM((R, CELL_COLS * size), BF16)],
    )(vert, horiz, *strips, *aboves, *belows)
    return coadd[None], detect[None]


def solution(mesh):
    in_specs = (
        P(("visit", "patch"), None, None),
        P(("visit", "patch"), None),
        P(("visit", "patch")),
        P(("visit", "patch")),
        P(("visit", "patch")),
        P(("visit", "patch")),
        P(),
        P(),
    )
    out_specs = (P("patch", "visit", None), P("patch", "visit", None))
    return jax.shard_map(shards, mesh=mesh, in_specs=in_specs, out_specs=out_specs, check_vma=False)
```

time: 613 us -> 100 us (0.16)
  the two profiles are of different devices: /device:TPU:8 before, /device:TPU:5 now
where the time goes in v1:
time: 100 us; the launch traced here: 99.9 us
  Pallas kernels  43.1 us (43%)
  starting transfers between devices  33.9 us (34%)
  waiting for transfers between devices  10.3 us (10%)
  local copies, waits for them, and re-layouts  8.98 us (9%)
  other arithmetic  2.7 us (3%)
    pallas_call x2, Pallas kernels, shards(): pl.pallas_call(functools.partial(match_kernel, cfg=cfg, cols_a=cols_a, co...  23.1 us
    ppermute x17, starting transfers between devices, send(): return lax.ppermute(value, ('visit', 'patch'), pairs)  17.7 us
    ppermute x2, starting transfers between devices, shards(): lax.ppermute(v, 'visit', [(i, i + 1) for i in range(V - 1)])  12.4 us
    ppermute x17, waiting for transfers between devices, send(): return lax.ppermute(value, ('visit', 'patch'), pairs)  8.86 us
    unnamed x48, local copies, waits for them, and re-layouts  6.8 us
    pallas_call x2, Pallas kernels, shards(): pl.pallas_call(functools.partial(first_add_kernel, cfg=cfg, na=na, nbc=nb...  5.26 us
    pallas_call x2, Pallas kernels, shards(): pl.pallas_call(functools.partial(second_add_kernel, cfg=cfg, na=na, nbc=n...  4.15 us
    pallas_call x2, Pallas kernels, shards(): pl.pallas_call(functools.partial(coadd_kernel, cfg=cfg, h0=cols_a[0], nh=...  3.89 us
  transfers between devices with their start and end apart: 21, of which 3 were waited for; matrix products, arithmetic and copies ran while one was open for 5% of the time, Pallas kernels for 29%

profile of v1, /device:TPU:5, one launch (start us, length us, event | category | flops | bytes accessed | tf_op | source)
XLA Modules:
  0.0 99.9 jit_solution(439423122051113169)
XLA Ops:
  0.6 0.7 collective-permute-start.2
  1.4 0.1 pad.2.clone
  1.4 0.7 multiply_reduce-precision_fusion.1
  2.1 0.7 multiply_reduce-precision_fusion
  2.8 0.1 maximum_maximum_fusion
  2.9 0.1 copy.10
  3.0 0.1 reshape.20.info_own
  3.1 0.1 collective-permute-start.1
  3.2 0.7 multiply_add_fusion.keys_own
  3.8 0.5 collective-permute-start
  4.3 0.6 pad_add_fusion.scal
  4.9 1.3 %reshape.26.taps = f32[210]{0:T(256)} reshape(bf16[5,2,21]{2,1,0:T(2,128)(2,1)} %param.14) | data formatting | bytes 1260 | tf_op jit(solution)/shard_map/reshape | solution.py:353
  6.3 2.4 %shard_map.96 = (bf16[640,128]{1,0:T(8,128)(2,1)}, bf16[640,128]{1,0:T(8,128)(2,1)}) custom-call(f32[210]{0:T(256)} %reshape.26.taps), custom_call_target="tpu_custom_call" | custom-call | tf_op jit(solution)/shard_map/pallas_call | solution.py:348
  8.7 0.5 copy-done.22
  9.2 0.1 copy-done.20
  9.2 0.8 copy-done
  10.0 11.9 %shard_map.101 = (bf16[2064,128]{1,0:T(8,128)(2,1)}, bf16[2064,128]{1,0:T(8,128)(2,1)}, bf16[2048,128]{1,0:T(8,128)(2,1)}, bf16[2048,128]{1,0:T(8,128)(2,1)}) custom-call(s32[4]{0:T(128)} %pad_add_fusion.scal, s32[64]{0:T(128)} %copy-done.21, s32[64]{0:T(128)} %copy-done.22, f32[512]{0:T(512)} %copy-done.19, f32[512]{0:T(512)} %copy-done.20, ...), custom_call_target="tpu_custom_call" | custom-call | tf_op jit(solution)/shard_map/pallas_call | solution.py:368
  21.9 1.9 %collective-permute-start.10 = (bf16[2064,128]{1,0:T(8,128)(2,1)}, bf16[2064,128]{1,0:T(8,128)(2,1)S(1)}, u32[]{:S(2)}, u32[]{:S(2)}) collective-permute-start(bf16[2064,128]{1,0:T(8,128)(2,1)} %get-tuple-element.56), channel_id=1, source_target_pairs={{0,2},{1,3},{2,0},{3,1},{4,6},{5,7},{6,4},{7,5},{8,10},{9,11},{10,... | collective-permute-start | bytes 1585160 | tf_op jit(solution)/shard_map/ppermute | solution.py:320
  23.8 0.9 collective-permute-start.11
  24.7 11.2 %shard_map.97 = (bf16[2064,128]{1,0:T(8,128)(2,1)}, bf16[2064,128]{1,0:T(8,128)(2,1)}, bf16[2048,128]{1,0:T(8,128)(2,1)}, bf16[2048,128]{1,0:T(8,128)(2,1)}) custom-call(s32[4]{0:T(128)} %pad_add_fusion.scal, s32[64]{0:T(128)} %copy-done.21, s32[64]{0:T(128)} %copy-done.22, f32[512]{0:T(512)} %copy-done.19, f32[512]{0:T(512)} %copy-done.20, ...), custom_call_target="tpu_custom_call" | custom-call | tf_op jit(solution)/shard_map/pallas_call | solution.py:368
  35.9 1.4 %collective-permute-start.3 = (bf16[2064,128]{1,0:T(8,128)(2,1)}, bf16[2064,128]{1,0:T(8,128)(2,1)S(1)}, u32[]{:S(2)}, u32[]{:S(2)}) collective-permute-start(bf16[2064,128]{1,0:T(8,128)(2,1)} %get-tuple-element.43), channel_id=1, source_target_pairs={{0,2},{1,3},{2,0},{3,1},{4,6},{5,7},{6,4},{7,5},{8,10},{9,11},{10,... | collective-permute-start | bytes 1585160 | tf_op jit(solution)/shard_map/ppermute | solution.py:320
  37.4 0.8 copy-done.4
  38.1 0.2 copy-done.2
  38.3 2.6 %shard_map.102 = (bf16[1040,128]{1,0:T(8,128)(2,1)}, bf16[1040,128]{1,0:T(8,128)(2,1)}, bf16[1024,128]{1,0:T(8,128)(2,1)}, bf16[1024,128]{1,0:T(8,128)(2,1)}) custom-call(s32[4]{0:T(128)} %pad_add_fusion.scal, bf16[2064,128]{1,0:T(8,128)(2,1)} %get-tuple-element.55.refs_0_, bf16[2064,128]{1,0:T(8,128)(2,1)} %copy-done.2, ...), custom_call_target="tpu_custom_call" | custom-call | tf_op jit(solution)/shard_map/pallas_call | solution.py:398
  40.9 1.5 %collective-permute-start.12 = (bf16[1040,128]{1,0:T(8,128)(2,1)}, bf16[1040,128]{1,0:T(8,128)(2,1)S(1)}, u32[]{:S(2)}, u32[]{:S(2)}) collective-permute-start(bf16[1040,128]{1,0:T(8,128)(2,1)} %get-tuple-element.60), channel_id=1, source_target_pairs={{0,4},{1,5},{2,6},{3,7},{4,0},{5,1},{6,2},{7,3},{8,12},{9,13},{10,... | collective-permute-start | bytes 798728 | tf_op jit(solution)/shard_map/ppermute | solution.py:320
  42.4 0.1 collective-permute-start.13
  42.5 6.3 %collective-permute-done.4.refs_3_ = bf16[2048,128]{1,0:T(8,128)(2,1)S(1)} collective-permute-done((bf16[2048,128]{1,0:T(8,128)(2,1)}, bf16[2048,128]{1,0:T(8,128)(2,1)S(1)}, u32[]{:S(2)}, u32[]{:S(2)}) %collective-permute-start.4) | collective-permute-done | bytes 524320 | tf_op jit(solution)/shard_map/ppermute | solution.py:320
  48.8 0.8 copy-done.3
  49.6 0.2 copy-done.1
  49.8 2.6 %shard_map.98 = (bf16[1040,128]{1,0:T(8,128)(2,1)}, bf16[1040,128]{1,0:T(8,128)(2,1)}, bf16[1024,128]{1,0:T(8,128)(2,1)}, bf16[1024,128]{1,0:T(8,128)(2,1)}) custom-call(s32[4]{0:T(128)} %pad_add_fusion.scal, bf16[2064,128]{1,0:T(8,128)(2,1)} %get-tuple-element.42.refs_0_, bf16[2064,128]{1,0:T(8,128)(2,1)} %copy-done.1, ...), custom_call_target="tpu_custom_call" | custom-call | tf_op jit(solution)/shard_map/pallas_call | solution.py:398
  52.4 1.0 collective-permute-start.5
  53.4 0.7 collective-permute-start.6
  54.2 0.0 copy-start.6
  54.2 0.7 copy-done.8
  54.9 0.1 copy-done.6
  54.9 2.1 %shard_map.103 = (bf16[528,128]{1,0:T(8,128)(2,1)}, bf16[528,128]{1,0:T(8,128)(2,1)}, bf16[528,128]{1,0:T(8,128)(2,1)}, bf16[528,128]{1,0:T(8,128)(2,1)}) custom-call(s32[4]{0:T(128)} %pad_add_fusion.scal, bf16[1040,128]{1,0:T(8,128)(2,1)} %get-tuple-element.59.refs_0_, bf16[1040,128]{1,0:T(8,128)(2,1)} %copy-done.6, ...), custom_call_target="tpu_custom_call" | custom-call | tf_op jit(solution)/shard_map/pallas_call | solution.py:409
  57.0 1.7 %collective-permute-start.14 = (bf16[528,128]{1,0:T(8,128)(2,1)}, bf16[528,128]{1,0:T(8,128)(2,1)S(1)}, u32[]{:S(2)}, u32[]{:S(2)}) collective-permute-start(bf16[528,128]{1,0:T(8,128)(2,1)} %get-tuple-element.64), channel_id=1, source_target_pairs={{0,8},{1,9},{2,10},{3,11},{4,12},{5,13},{6,14},{7,15},{8,16},{9,17... | collective-permute-start | bytes 405512 | tf_op jit(solution)/shard_map/ppermute | solution.py:320
  58.7 2.2 %collective-permute-start.15 = (bf16[528,128]{1,0:T(8,128)(2,1)}, bf16[528,128]{1,0:T(8,128)(2,1)S(1)}, u32[]{:S(2)}, u32[]{:S(2)}) collective-permute-start(bf16[528,128]{1,0:T(8,128)(2,1)} %get-tuple-element.65), channel_id=1, source_target_pairs={{0,16},{1,17},{2,18},{3,19},{4,20},{5,21},{6,22},{7,23},{8,24},{9,... | collective-permute-start | bytes 405512 | tf_op jit(solution)/shard_map/ppermute | solution.py:320
  60.9 1.7 %collective-permute-start.16 = (bf16[528,128]{1,0:T(8,128)(2,1)}, bf16[528,128]{1,0:T(8,128)(2,1)S(1)}, u32[]{:S(2)}, u32[]{:S(2)}) collective-permute-start(bf16[528,128]{1,0:T(8,128)(2,1)} %get-tuple-element.66), channel_id=1, source_target_pairs={{0,24},{1,25},{2,26},{3,27},{4,28},{5,29},{6,30},{7,31},{8,0},{9,1... | collective-permute-start | bytes 405512 | tf_op jit(solution)/shard_map/ppermute | solution.py:320
  62.6 0.0 copy-start.5
  62.6 0.7 copy-done.7
  63.3 0.1 copy-done.5
  63.4 2.1 %shard_map.99 = (bf16[528,128]{1,0:T(8,128)(2,1)}, bf16[528,128]{1,0:T(8,128)(2,1)}, bf16[528,128]{1,0:T(8,128)(2,1)}, bf16[528,128]{1,0:T(8,128)(2,1)}) custom-call(s32[4]{0:T(128)} %pad_add_fusion.scal, bf16[1040,128]{1,0:T(8,128)(2,1)} %get-tuple-element.46.refs_0_, bf16[1040,128]{1,0:T(8,128)(2,1)} %copy-done.5, ...), custom_call_target="tpu_custom_call" | custom-call | tf_op jit(solution)/shard_map/pallas_call | solution.py:409
  65.5 0.3 collective-permute-start.8
  65.8 3.0 %collective-permute-start.9 = (bf16[528,128]{1,0:T(8,128)(2,1)}, bf16[528,128]{1,0:T(8,128)(2,1)S(1)}, u32[]{:S(2)}, u32[]{:S(2)}) collective-permute-start(bf16[528,128]{1,0:T(8,128)(2,1)} %get-tuple-element.53), channel_id=1, source_target_pairs={{0,24},{1,25},{2,26},{3,27},{4,28},{5,29},{6,30},{7,31},{8,0},{9,1... | collective-permute-start | bytes 405512 | tf_op jit(solution)/shard_map/ppermute | solution.py:320
  68.8 2.5 %collective-permute-done.15.refs_2_ = bf16[528,128]{1,0:T(8,128)(2,1)S(1)} collective-permute-done((bf16[528,128]{1,0:T(8,128)(2,1)}, bf16[528,128]{1,0:T(8,128)(2,1)S(1)}, u32[]{:S(2)}, u32[]{:S(2)}) %collective-permute-start.15) | collective-permute-done | bytes 135200 | tf_op jit(solution)/shard_map/ppermute | solution.py:320
  71.3 0.6 copy-done.11
  71.9 0.0 copy-done.13
  72.0 1.9 %shard_map.104 = (f32[128,512]{1,0:T(8,128)}, bf16[32,512]{1,0:T(8,128)(2,1)}, bf16[32,512]{1,0:T(8,128)(2,1)}) custom-call(s32[4]{0:T(128)} %pad_add_fusion.scal, bf16[528,128]{1,0:T(8,128)(2,1)} %get-tuple-element.63.refs_0_, bf16[528,128]{1,0:T(8,128)(2,1)} %copy-done.9, bf16[528,128]{1,0:T(8,128)(2,1)} %copy-done.11, bf16[528,128]{1,0:T(8,128)(2,1)} %copy-done.13), custom_call_target="tpu_custom_call" | custom-call | tf_op jit(solution)/shard_map/pallas_call | solution.py:416
  73.9 8.2 %collective-permute-start.18 = (bf16[32,512]{1,0:T(8,128)(2,1)}, bf16[32,512]{1,0:T(8,128)(2,1)S(1)}, u32[]{:S(2)}, u32[]{:S(2)}) collective-permute-start(bf16[32,512]{1,0:T(8,128)(2,1)} %get-tuple-element.69), channel_id=1, source_target_pairs={{0,4},{4,8},{8,12},{12,16},{16,20},{20,24},{24,28},{1,5},{5,9},{9,... | collective-permute-start | bytes 98312 | tf_op jit(solution)/shard_map/ppermute | solution.py:429
  82.1 1.9 %collective-permute-start.20 = (bf16[32,512]{1,0:T(8,128)(2,1)}, bf16[32,512]{1,0:T(8,128)(2,1)S(1)}, u32[]{:S(2)}, u32[]{:S(2)}) collective-permute-start(bf16[32,512]{1,0:T(8,128)(2,1)} %get-tuple-element.71), channel_id=1, source_target_pairs={{4,0},{8,4},{12,8},{16,12},{20,16},{24,20},{28,24},{5,1},{9,5},{13... | collective-permute-start | bytes 98312 | tf_op jit(solution)/shard_map/ppermute | solution.py:430
  84.0 0.0 copy-start.10
  84.0 0.0 copy-start.12
  84.1 0.6 copy-done.10
  84.7 0.0 copy-done.12
  84.7 0.0 copy-done.14
  84.8 2.0 %shard_map.100 = (f32[128,512]{1,0:T(8,128)}, bf16[32,512]{1,0:T(8,128)(2,1)}, bf16[32,512]{1,0:T(8,128)(2,1)}) custom-call(s32[4]{0:T(128)} %pad_add_fusion.scal, bf16[528,128]{1,0:T(8,128)(2,1)} %get-tuple-element.50.refs_0_, bf16[528,128]{1,0:T(8,128)(2,1)} %copy-done.10, bf16[528,128]{1,0:T(8,128)(2,1)} %copy-done.12, bf16[528,128]{1,0:T(8,128)(2,1)} %copy-done.14), custom_call_target="tpu_custom_call" | custom-call | tf_op jit(solution)/shard_map/pallas_call | solution.py:416
  86.7 4.2 %collective-permute-start.17 = (bf16[32,512]{1,0:T(8,128)(2,1)}, bf16[32,512]{1,0:T(8,128)(2,1)S(1)}, u32[]{:S(2)}, u32[]{:S(2)}) collective-permute-start(bf16[32,512]{1,0:T(8,128)(2,1)} %get-tuple-element.68), channel_id=1, source_target_pairs={{0,4},{4,8},{8,12},{12,16},{16,20},{20,24},{24,28},{1,5},{5,9},{9,... | collective-permute-start | bytes 98312 | tf_op jit(solution)/shard_map/ppermute | solution.py:429
  91.0 1.9 %collective-permute-start.19 = (bf16[32,512]{1,0:T(8,128)(2,1)}, bf16[32,512]{1,0:T(8,128)(2,1)S(1)}, u32[]{:S(2)}, u32[]{:S(2)}) collective-permute-start(bf16[32,512]{1,0:T(8,128)(2,1)} %get-tuple-element.70), channel_id=1, source_target_pairs={{4,0},{8,4},{12,8},{16,12},{20,16},{24,20},{28,24},{5,1},{9,5},{13... | collective-permute-start | bytes 98312 | tf_op jit(solution)/shard_map/ppermute | solution.py:430
  92.9 0.6 reshape.24.taps
  93.5 1.7 %shard_map.95 = (bf16[128,192]{1,0:T(8,128)(2,1)}, bf16[384,128]{1,0:T(8,128)(2,1)}) custom-call(f32[82]{0:T(128)} %reshape.24.taps), custom_call_target="tpu_custom_call" | custom-call | tf_op jit(solution)/shard_map/pallas_call | solution.py:354
  95.3 1.4 %collective-permute-done.19.refs_4_ = bf16[32,512]{1,0:T(8,128)(2,1)S(1)} collective-permute-done((bf16[32,512]{1,0:T(8,128)(2,1)}, bf16[32,512]{1,0:T(8,128)(2,1)S(1)}, u32[]{:S(2)}, u32[]{:S(2)}) %collective-permute-start.19) | collective-permute-done | bytes 32800 | tf_op jit(solution)/shard_map/ppermute | solution.py:430
  96.8 0.6 copy-done.18
  97.4 2.6 %shard_map.105 = (f32[128,1024]{1,0:T(8,128)}, f32[128,1024]{1,0:T(8,128)}) custom-call(bf16[128,192]{1,0:T(8,128)(2,1)} %get-tuple-element.38.vert, bf16[384,128]{1,0:T(8,128)(2,1)} %get-tuple-element.39.horiz, f32[128,512]{1,0:T(8,128)} %get-tuple-element.54.refs_0_, f32[128,512]{1,0:T(8,128)} %get-tuple-element.67.refs_1_, bf16[32,512]{1,0:T(8,128)(2,1)} %copy-done.17, ...), custom_call_target="tpu_custom_call" | custom-call | tf_op jit(solution)/shard_map/pallas_call | solution.py:432
  (48 shorter events, 0.1 us)
Async XLA Ops:
  0.6 8.0 %collective-permute-start.2 = (bf16[64,128,128]{2,1,0:T(8,128)(2,1)}, bf16[64,128,128]{2,1,0:T(8,128)(2,1)S(1)}, u32[]{:S(2)}, u32[]{:S(2)}) collective-permute-start(bf16[64,128,128]{2,1,0:T(8,128)(2,1)} %tiles_own.3), channel_id=1, source_target_pairs={{0,1},{1,0},{2,3},{3,2},{4,5},{5,4},{6,7},{7,6},{8,9},{9,8},{10,11... | collective-permute-start | bytes 6291464 | tf_op jit(solution)/shard_map/ppermute | solution.py:320
  3.1 5.6 %copy-start.19 = (f32[512]{0:T(512)}, f32[512]{0:T(512)S(1)}, u32[]{:S(2)}) copy-start(f32[512]{0:T(512)S(1)} %reshape.20.info_own) | copy-start | bytes 6148
  3.1 5.6 %collective-permute-start.1 = (f32[512]{0:T(512)S(1)}, f32[512]{0:T(512)S(1)}, u32[]{:S(2)}, u32[]{:S(2)}) collective-permute-start(f32[512]{0:T(512)S(1)} %reshape.20.info_own), channel_id=1, source_target_pairs={{0,1},{1,0},{2,3},{3,2},{4,5},{5,4},{6,7},{7,6},{8,9},{9,8},{10,11... | collective-permute-start | bytes 6152 | tf_op jit(solution)/shard_map/ppermute | solution.py:320
  3.8 4.8 %copy-start.21 = (s32[64]{0:T(128)}, s32[64]{0:T(128)S(1)}, u32[]{:S(2)}) copy-start(s32[64]{0:T(128)S(1)} %multiply_add_fusion.keys_own) | copy-start | bytes 772
  3.8 4.8 %collective-permute-start = (s32[64]{0:T(128)S(1)}, s32[64]{0:T(128)S(1)}, u32[]{:S(2)}, u32[]{:S(2)}) collective-permute-start(s32[64]{0:T(128)S(1)} %multiply_add_fusion.keys_own), channel_id=1, source_target_pairs={{0,1},{1,0},{2,3},{3,2},{4,5},{5,4},{6,7},{7,6},{8,9},{9,8},{10,11... | collective-permute-start | bytes 776 | tf_op jit(solution)/shard_map/ppermute | solution.py:320
  8.6 0.5 copy-start.22
  8.6 0.6 copy-start.20
  8.7 1.3 %copy-start = (bf16[64,128,128]{2,1,0:T(8,128)(2,1)}, bf16[64,128,128]{2,1,0:T(8,128)(2,1)S(1)}, u32[]{:S(2)}) copy-start(bf16[64,128,128]{2,1,0:T(8,128)(2,1)S(1)} %collective-permute-done.2.tiles_other) | copy-start | bytes 6291460
  21.9 15.5 %collective-permute-start.10 = (bf16[2064,128]{1,0:T(8,128)(2,1)}, bf16[2064,128]{1,0:T(8,128)(2,1)S(1)}, u32[]{:S(2)}, u32[]{:S(2)}) collective-permute-start(bf16[2064,128]{1,0:T(8,128)(2,1)} %get-tuple-element.56), channel_id=1, source_target_pairs={{0,2},{1,3},{2,0},{3,1},{4,6},{5,7},{6,4},{7,5},{8,10},{9,11},{10,... | collective-permute-start | bytes 1585160 | tf_op jit(solution)/shard_map/ppermute | solution.py:320
  23.8 13.5 %collective-permute-start.11 = (bf16[2048,128]{1,0:T(8,128)(2,1)}, bf16[2048,128]{1,0:T(8,128)(2,1)S(1)}, u32[]{:S(2)}, u32[]{:S(2)}) collective-permute-start(bf16[2048,128]{1,0:T(8,128)(2,1)} %get-tuple-element.58), channel_id=1, source_target_pairs={{0,4},{1,5},{2,6},{3,7},{4,0},{5,1},{6,2},{7,3},{8,12},{9,13},{10,... | collective-permute-start | bytes 1572872 | tf_op jit(solution)/shard_map/ppermute | solution.py:320
  35.9 12.9 %collective-permute-start.3 = (bf16[2064,128]{1,0:T(8,128)(2,1)}, bf16[2064,128]{1,0:T(8,128)(2,1)S(1)}, u32[]{:S(2)}, u32[]{:S(2)}) collective-permute-start(bf16[2064,128]{1,0:T(8,128)(2,1)} %get-tuple-element.43), channel_id=1, source_target_pairs={{0,2},{1,3},{2,0},{3,1},{4,6},{5,7},{6,4},{7,5},{8,10},{9,11},{10,... | collective-permute-start | bytes 1585160 | tf_op jit(solution)/shard_map/ppermute | solution.py:320
  37.3 11.5 %collective-permute-start.4 = (bf16[2048,128]{1,0:T(8,128)(2,1)}, bf16[2048,128]{1,0:T(8,128)(2,1)S(1)}, u32[]{:S(2)}, u32[]{:S(2)}) collective-permute-start(bf16[2048,128]{1,0:T(8,128)(2,1)} %get-tuple-element.45), channel_id=1, source_target_pairs={{0,4},{1,5},{2,6},{3,7},{4,0},{5,1},{6,2},{7,3},{8,12},{9,13},{10,... | collective-permute-start | bytes 1572872 | tf_op jit(solution)/shard_map/ppermute | solution.py:320
  37.3 0.8 copy-start.4
  37.3 1.0 copy-start.2
  40.9 13.2 %collective-permute-start.12 = (bf16[1040,128]{1,0:T(8,128)(2,1)}, bf16[1040,128]{1,0:T(8,128)(2,1)S(1)}, u32[]{:S(2)}, u32[]{:S(2)}) collective-permute-start(bf16[1040,128]{1,0:T(8,128)(2,1)} %get-tuple-element.60), channel_id=1, source_target_pairs={{0,4},{1,5},{2,6},{3,7},{4,0},{5,1},{6,2},{7,3},{8,12},{9,13},{10,... | collective-permute-start | bytes 798728 | tf_op jit(solution)/shard_map/ppermute | solution.py:320
  42.4 11.8 %collective-permute-start.13 = (bf16[1024,128]{1,0:T(8,128)(2,1)}, bf16[1024,128]{1,0:T(8,128)(2,1)S(1)}, u32[]{:S(2)}, u32[]{:S(2)}) collective-permute-start(bf16[1024,128]{1,0:T(8,128)(2,1)} %get-tuple-element.62), channel_id=1, source_target_pairs={{0,2},{1,3},{2,0},{3,1},{4,6},{5,7},{6,4},{7,5},{8,10},{9,11},{10,... | collective-permute-start | bytes 786440 | tf_op jit(solution)/shard_map/ppermute | solution.py:320
  48.8 0.8 copy-start.3
  48.8 1.0 copy-start.1
  52.4 40.5 %copy-start.23 = (bf16[2,41]{1,0:T(2,128)(2,1)S(1)}, bf16[2,41]{1,0:T(2,128)(2,1)}, u32[]{:S(2)}) copy-start(bf16[2,41]{1,0:T(2,128)(2,1)} %param.15) | copy-start | bytes 496
  52.4 10.1 %collective-permute-start.5 = (bf16[1040,128]{1,0:T(8,128)(2,1)}, bf16[1040,128]{1,0:T(8,128)(2,1)S(1)}, u32[]{:S(2)}, u32[]{:S(2)}) collective-permute-start(bf16[1040,128]{1,0:T(8,128)(2,1)} %get-tuple-element.47), channel_id=1, source_target_pairs={{0,4},{1,5},{2,6},{3,7},{4,0},{5,1},{6,2},{7,3},{8,12},{9,13},{10,... | collective-permute-start | bytes 798728 | tf_op jit(solution)/shard_map/ppermute | solution.py:320
  53.4 9.2 %collective-permute-start.6 = (bf16[1024,128]{1,0:T(8,128)(2,1)}, bf16[1024,128]{1,0:T(8,128)(2,1)S(1)}, u32[]{:S(2)}, u32[]{:S(2)}) collective-permute-start(bf16[1024,128]{1,0:T(8,128)(2,1)} %get-tuple-element.49), channel_id=1, source_target_pairs={{0,2},{1,3},{2,0},{3,1},{4,6},{5,7},{6,4},{7,5},{8,10},{9,11},{10,... | collective-permute-start | bytes 786440 | tf_op jit(solution)/shard_map/ppermute | solution.py:320
  54.1 0.7 copy-start.8
  54.2 0.8 copy-start.6
  57.0 8.7 %collective-permute-start.14 = (bf16[528,128]{1,0:T(8,128)(2,1)}, bf16[528,128]{1,0:T(8,128)(2,1)S(1)}, u32[]{:S(2)}, u32[]{:S(2)}) collective-permute-start(bf16[528,128]{1,0:T(8,128)(2,1)} %get-tuple-element.64), channel_id=1, source_target_pairs={{0,8},{1,9},{2,10},{3,11},{4,12},{5,13},{6,14},{7,15},{8,16},{9,17... | collective-permute-start | bytes 405512 | tf_op jit(solution)/shard_map/ppermute | solution.py:320
  58.7 12.5 %collective-permute-start.15 = (bf16[528,128]{1,0:T(8,128)(2,1)}, bf16[528,128]{1,0:T(8,128)(2,1)S(1)}, u32[]{:S(2)}, u32[]{:S(2)}) collective-permute-start(bf16[528,128]{1,0:T(8,128)(2,1)} %get-tuple-element.65), channel_id=1, source_target_pairs={{0,16},{1,17},{2,18},{3,19},{4,20},{5,21},{6,22},{7,23},{8,24},{9,... | collective-permute-start | bytes 405512 | tf_op jit(solution)/shard_map/ppermute | solution.py:320
  60.9 10.4 %collective-permute-start.16 = (bf16[528,128]{1,0:T(8,128)(2,1)}, bf16[528,128]{1,0:T(8,128)(2,1)S(1)}, u32[]{:S(2)}, u32[]{:S(2)}) collective-permute-start(bf16[528,128]{1,0:T(8,128)(2,1)} %get-tuple-element.66), channel_id=1, source_target_pairs={{0,24},{1,25},{2,26},{3,27},{4,28},{5,29},{6,30},{7,31},{8,0},{9,1... | collective-permute-start | bytes 405512 | tf_op jit(solution)/shard_map/ppermute | solution.py:320
  62.6 0.7 copy-start.7
  62.6 0.8 copy-start.5
  65.5 18.6 %collective-permute-start.7 = (bf16[528,128]{1,0:T(8,128)(2,1)}, bf16[528,128]{1,0:T(8,128)(2,1)S(1)}, u32[]{:S(2)}, u32[]{:S(2)}) collective-permute-start(bf16[528,128]{1,0:T(8,128)(2,1)} %get-tuple-element.51), channel_id=1, source_target_pairs={{0,8},{1,9},{2,10},{3,11},{4,12},{5,13},{6,14},{7,15},{8,16},{9,17... | collective-permute-start | bytes 405512 | tf_op jit(solution)/shard_map/ppermute | solution.py:320
  65.5 18.6 %collective-permute-start.8 = (bf16[528,128]{1,0:T(8,128)(2,1)}, bf16[528,128]{1,0:T(8,128)(2,1)S(1)}, u32[]{:S(2)}, u32[]{:S(2)}) collective-permute-start(bf16[528,128]{1,0:T(8,128)(2,1)} %get-tuple-element.52), channel_id=1, source_target_pairs={{0,16},{1,17},{2,18},{3,19},{4,20},{5,21},{6,22},{7,23},{8,24},{9,... | collective-permute-start | bytes 405512 | tf_op jit(solution)/shard_map/ppermute | solution.py:320
  65.7 5.5 %copy-start.9 = (bf16[528,128]{1,0:T(8,128)(2,1)}, bf16[528,128]{1,0:T(8,128)(2,1)S(1)}, u32[]{:S(2)}) copy-start(bf16[528,128]{1,0:T(8,128)(2,1)S(1)} %collective-permute-done.14.refs_1_) | copy-start | bytes 405508
  65.8 18.3 %collective-permute-start.9 = (bf16[528,128]{1,0:T(8,128)(2,1)}, bf16[528,128]{1,0:T(8,128)(2,1)S(1)}, u32[]{:S(2)}, u32[]{:S(2)}) collective-permute-start(bf16[528,128]{1,0:T(8,128)(2,1)} %get-tuple-element.53), channel_id=1, source_target_pairs={{0,24},{1,25},{2,26},{3,27},{4,28},{5,29},{6,30},{7,31},{8,0},{9,1... | collective-permute-start | bytes 405512 | tf_op jit(solution)/shard_map/ppermute | solution.py:320
  71.3 0.7 copy-start.11
  71.3 0.7 copy-start.13
  73.9 21.4 %collective-permute-start.18 = (bf16[32,512]{1,0:T(8,128)(2,1)}, bf16[32,512]{1,0:T(8,128)(2,1)S(1)}, u32[]{:S(2)}, u32[]{:S(2)}) collective-permute-start(bf16[32,512]{1,0:T(8,128)(2,1)} %get-tuple-element.69), channel_id=1, source_target_pairs={{0,4},{4,8},{8,12},{12,16},{16,20},{20,24},{24,28},{1,5},{5,9},{9,... | collective-permute-start | bytes 98312 | tf_op jit(solution)/shard_map/ppermute | solution.py:429
  82.1 13.2 %collective-permute-start.20 = (bf16[32,512]{1,0:T(8,128)(2,1)}, bf16[32,512]{1,0:T(8,128)(2,1)S(1)}, u32[]{:S(2)}, u32[]{:S(2)}) collective-permute-start(bf16[32,512]{1,0:T(8,128)(2,1)} %get-tuple-element.71), channel_id=1, source_target_pairs={{4,0},{8,4},{12,8},{16,12},{20,16},{24,20},{28,24},{5,1},{9,5},{13... | collective-permute-start | bytes 98312 | tf_op jit(solution)/shard_map/ppermute | solution.py:430
  84.0 0.7 copy-start.10
  84.0 0.7 copy-start.12
  84.1 0.7 copy-start.14
  86.7 8.6 %collective-permute-start.17 = (bf16[32,512]{1,0:T(8,128)(2,1)}, bf16[32,512]{1,0:T(8,128)(2,1)S(1)}, u32[]{:S(2)}, u32[]{:S(2)}) collective-permute-start(bf16[32,512]{1,0:T(8,128)(2,1)} %get-tuple-element.68), channel_id=1, source_target_pairs={{0,4},{4,8},{8,12},{12,16},{16,20},{20,24},{24,28},{1,5},{5,9},{9,... | collective-permute-start | bytes 98312 | tf_op jit(solution)/shard_map/ppermute | solution.py:429
  91.0 5.8 %collective-permute-start.19 = (bf16[32,512]{1,0:T(8,128)(2,1)}, bf16[32,512]{1,0:T(8,128)(2,1)S(1)}, u32[]{:S(2)}, u32[]{:S(2)}) collective-permute-start(bf16[32,512]{1,0:T(8,128)(2,1)} %get-tuple-element.70), channel_id=1, source_target_pairs={{4,0},{8,4},{12,8},{16,12},{20,16},{24,20},{28,24},{5,1},{9,5},{13... | collective-permute-start | bytes 98312 | tf_op jit(solution)/shard_map/ppermute | solution.py:430
  95.3 1.5 %copy-start.15 = (bf16[32,512]{1,0:T(8,128)(2,1)}, bf16[32,512]{1,0:T(8,128)(2,1)S(1)}, u32[]{:S(2)}) copy-start(bf16[32,512]{1,0:T(8,128)(2,1)S(1)} %collective-permute-done.18.refs_3_) | copy-start | bytes 98308
  95.3 1.5 %copy-start.16 = (bf16[32,512]{1,0:T(8,128)(2,1)}, bf16[32,512]{1,0:T(8,128)(2,1)S(1)}, u32[]{:S(2)}) copy-start(bf16[32,512]{1,0:T(8,128)(2,1)S(1)} %collective-permute-done.20.refs_5_) | copy-start | bytes 98308
  95.3 1.5 %copy-start.17 = (bf16[32,512]{1,0:T(8,128)(2,1)}, bf16[32,512]{1,0:T(8,128)(2,1)S(1)}, u32[]{:S(2)}) copy-start(bf16[32,512]{1,0:T(8,128)(2,1)S(1)} %collective-permute-done.17.refs_2_) | copy-start | bytes 98308
  96.8 0.6 copy-start.18

commit v2 on v0

v2 whole, which is shorter than its diff:
```python
import functools

import jax
import jax.numpy as jnp
from jax import lax
from jax.experimental import pallas as pl
from jax.experimental.pallas import tpu as pltpu
from jax.sharding import PartitionSpec as P

CELL_ROWS = 8
CELL_COLS = 8
CELLS = CELL_ROWS * CELL_COLS
SETS = ((0, 4), (4, 8))
UNROLL = 8
EDGE = 32
WKEEP = 8
WSEND = 32
F32 = jnp.float32
BF16 = jnp.bfloat16
VMEM = pl.BlockSpec(memory_space=pltpu.VMEM)
SMEM = pl.BlockSpec(memory_space=pltpu.SMEM)
ANY = pl.BlockSpec(memory_space=pl.ANY)


def rows_shape(rows, dtype=BF16):
    return jax.ShapeDtypeStruct((rows, 128), dtype)


def turned(row, ncols, shift):
    full = pltpu.roll(jnp.broadcast_to(row, (128, ncols)), shift % ncols, 1)
    return pltpu.roll(full, 0, 1, stride=1, stride_axis=0)


def mats_kernel(basis, filt, row_out, col_out, vert_out, horiz_out, *, nb, nt, nf, size, strip):
    reach = (nt - 1) // 2
    row = lax.broadcasted_iota(jnp.int32, (size, size), 0)
    col = lax.broadcasted_iota(jnp.int32, (size, size), 1)
    near = jnp.abs(col - row) <= reach
    for b in range(nb):
        block = slice(b * size, (b + 1) * size)
        taps = basis[b : b + 1, :]
        row_out[:, block] = jnp.where(near, turned(taps, size, -reach), 0.0).astype(BF16)
        taps = basis[nb + b : nb + b + 1, :]
        col_out[:, block] = jnp.where(near, turned(taps, size, -reach), 0.0).astype(BF16)
    reach = (nf - 1) // 2
    taps = jnp.concatenate([filt[0:1, :], jnp.zeros((1, 128), F32)], axis=1)
    vert_out[...] = turned(taps, 256, EDGE - reach)[:strip, : strip + 2 * EDGE].astype(BF16)
    for k in range(3):
        inside = jnp.abs((k - 1) * size + row - col) <= reach
        taps = jnp.where(inside, turned(filt[1:2, :], size, -reach), 0.0)
        horiz_out[k * size : (k + 1) * size, :] = taps.astype(BF16)


def pack_weights(w):
    hi = w.astype(BF16)
    rest = w - hi.astype(F32)
    mid = rest.astype(BF16)
    lo = (rest - mid.astype(F32)).astype(BF16)
    parts = [hi.astype(F32), mid.astype(F32), lo.astype(F32), jnp.zeros_like(w)]
    return jnp.concatenate(parts, axis=0).astype(BF16)


def unpack_weights(block):
    block = block.astype(F32)
    return block[0:8] + block[8:16] + block[16:24]


def pick(swap, a, b):
    return jnp.where(swap, b, a), jnp.where(swap, a, b)


def match_kernel(scal, info_own, info_other, tiles_own, tiles_other, row_cat, col_cat, *refs, cfg, h0, nh):
    X, Y, Z, R, nb, count, n1, n2 = cfg
    acc, wacc = refs[:2]
    sends = refs[2 : 1 + n1]
    listing, scaled, own_s, other_s, sems = refs[1 + n1 :]
    size = tiles_own.shape[1]
    parts = size // R
    x, core, y, swap = scal[0], scal[1], scal[3], scal[4] > 0
    loads = [
        pltpu.make_async_copy(info_own, own_s, sems.at[0]),
        pltpu.make_async_copy(info_other, other_s, sems.at[1]),
    ]
    for copy in loads:
        copy.start()
    acc[...] = jnp.zeros_like(acc)
    wacc[...] = jnp.zeros_like(wacc)
    scaled[1] = jnp.zeros_like(scaled[1])
    for copy in loads:
        copy.wait()

    def lister(info, base):
        def body(t, n):
            key = info[6, t].astype(jnp.int32)
            h = key & (CELL_COLS - 1)
            mine = (((key >> 6) & 1) == core) & (h >= h0) & (h < h0 + nh)
            listing[n] = base + t
            return n + mine.astype(jnp.int32)

        return body

    n = lax.fori_loop(0, count, lister(own_s, 0), jnp.int32(0), unroll=8)
    n = lax.fori_loop(0, count, lister(other_s, count), n, unroll=8)
    for q in range(UNROLL):
        listing[n + q] = 0
    lane = lax.broadcasted_iota(jnp.int32, (1, 128), 1)

    def fetch(k, what):
        t = listing[jnp.clip(k, 0, n)]
        own = t < count
        t_in = jnp.where(own, t, t - count)
        return own, t_in, [jnp.where(own, own_s[b, t_in], other_s[b, t_in]) for b in what]

    def step(i, carry):
        now = i & 1
        for q in range(0, UNROLL, 2):
            pair, tall = [], []
            for k in (i * UNROLL + q, i * UNROLL + q + 1):
                own, t, values = fetch(k, range(nb))
                pair.append([jnp.where(k < n, v, 0.0) for v in values])
                tall.append(jnp.where(own, tiles_own[t], tiles_other[t]))
            tall = jnp.concatenate(tall, axis=0)
            cols = jnp.dot(tall, col_cat[...], preferred_element_type=F32)
            for j, values in enumerate(pair):
                for b in range(nb):
                    part = cols[j * size : (j + 1) * size, b * size : (b + 1) * size] * values[b]
                    scaled[now, b * size : (b + 1) * size, (q + j) * size : (q + j + 1) * size] = (
                        part.astype(BF16)
                    )
        for q in range(0, UNROLL, 2):
            wide = scaled[1 - now, :, q * size : (q + 2) * size]
            out = jnp.dot(row_cat[...], wide, preferred_element_type=F32)
            for j in range(2):
                k = (i - 1) * UNROLL + q + j
                live = (k >= 0) & (k < n)
                _, _, (weight, key) = fetch(k, (nb, 6))
                key = jnp.where(live, key.astype(jnp.int32), h0)
                cell = key & (CELLS - 1)
                xp = key >> 7
                g = cell >> 3
                hh = (cell & (CELL_COLS - 1)) - h0
                for part in range(parts):
                    v = g * parts + part
                    spot = acc.at[xp, lax.rem(v, Y), v // Y, hh]
                    spot[...] = spot[...] + out[part * R : (part + 1) * R, j * size : (j + 1) * size]
                wrow = wacc.at[pl.ds(xp, 1), :]
                wrow[...] = wrow[...] + jnp.where((lane == cell) & live, weight, 0.0)
        return carry

    lax.fori_loop(0, (n + UNROLL - 1) // UNROLL + 1, step, jnp.int32(0))

    me = jnp.where(swap, y, x)
    block = Z * nh * R
    for i in range(1, n1):
        a = lax.rem(me + i, n1)
        for b in range(n2):
            xp, yp = pick(swap, a, b)
            for z in range(Z):
                for hh in range(nh):
                    start = b * block + (z * nh + hh) * R
                    sends[i - 1][start : start + R, :] = acc[xp, yp, z, hh].astype(BF16)
        sends[i - 1][n2 * block : n2 * block + WSEND, :] = pack_weights(wacc[...])


def first_add_kernel(scal, acc, wacc, *refs, cfg, nh):
    X, Y, Z, R, _, _, n1, n2 = cfg
    others = refs[: n1 - 1]
    keep, wkeep = refs[n1 - 1 : n1 + 1]
    sends = refs[n1 + 1 :]
    swap = scal[4] > 0
    first, second = jnp.where(swap, scal[3], scal[0]), jnp.where(swap, scal[0], scal[3])
    block = Z * nh * R
    w = wacc[...]
    for other in others:
        w = w + unpack_weights(other[n2 * block : n2 * block + WSEND])
    wkeep[...] = w
    for j in list(range(1, n2)) + [0]:
        b = lax.rem(second + j, n2)
        xp, yp = pick(swap, first, b)
        for z in range(Z):
            for hh in range(nh):
                at = (z * nh + hh) * R
                start = pl.multiple_of(b * block + at, 32)
                total = acc[xp, yp, z, hh]
                for other in others:
                    total = total + other[pl.ds(start, R), :].astype(F32)
                if j:
                    sends[j - 1][at : at + R, :] = total.astype(BF16)
                else:
                    keep[z, hh] = total
        if j:
            sends[j - 1][block : block + WSEND, :] = pack_weights(w)


def second_add_kernel(scal, kept, wkept, *refs, cfg, nh):
    X, Y, Z, R, _, _, n1, n2 = cfg
    others = refs[: n2 - 1]
    keep, wkeep = refs[n2 - 1 : n2 + 1]
    sends = refs[n2 + 1 :]
    w = wkept[...]
    for other in others:
        w = w + unpack_weights(other[Z * nh * R : Z * nh * R + WSEND])
    wkeep[...] = w
    for k in list(range(1, Z)) + [0]:
        z = lax.rem(scal[2] + k, Z)
        for hh in range(nh):
            start = pl.multiple_of((z * nh + hh) * R, 32)
            total = kept[z, hh]
            for other in others:
                total = total + other[pl.ds(start, R), :].astype(F32)
            if k:
                sends[k - 1][hh * R : (hh + 1) * R, :] = total.astype(BF16)
            else:
                keep[hh] = total
        if k:
            sends[k - 1][nh * R : nh * R + WSEND, :] = pack_weights(w)


def coadd_kernel(scal, kept, wkept, *refs, cfg, h0, nh, last):
    X, Y, Z, R = cfg[:4]
    others = refs[: Z - 1]
    befores = refs[Z - 1 : -3] if last else ()
    strip = refs[-3] if last else refs[-1]
    w = wkept[...]
    for other in others:
        w = w + unpack_weights(other[nh * R : nh * R + WSEND])
    g = (scal[2] * Y + scal[3]) // (Y * Z // CELL_ROWS)
    lane = lax.broadcasted_iota(jnp.int32, (WKEEP, 128), 1)
    patch = lax.broadcasted_iota(jnp.int32, (WKEEP, 128), 0)
    for hh in range(nh):
        total = kept[hh]
        for other in others:
            total = total + other[hh * R : (hh + 1) * R].astype(F32)
        here = (patch == scal[0]) & (lane == g * CELL_COLS + h0 + hh)
        denom = jnp.sum(jnp.where(here, w, 0.0)) + 1.0
        strip[:, hh * 128 : (hh + 1) * 128] = total / denom
    if last:
        top, bottom = refs[-2:]
        base = 0
        for part in list(befores) + [strip]:
            cols = slice(base, base + part.shape[1])
            top[:, cols] = part[:EDGE].astype(BF16)
            bottom[:, cols] = part[R - EDGE :].astype(BF16)
            base += part.shape[1]


def detect_kernel(vert, horiz, above, below, *refs):
    parts = refs[:-3]
    coadd, detect, filtered = refs[-3:]
    base = 0
    for part in parts:
        cols = slice(base, base + part.shape[1])
        coadd[:, cols] = part[...]
        extended = jnp.concatenate(
            [above[:, cols], part[...].astype(BF16), below[:, cols]], axis=0
        )
        filtered[:, cols] = jnp.dot(vert[...], extended, preferred_element_type=F32).astype(BF16)
        base += part.shape[1]
    blocks = base // 128
    for j in range(blocks):
        lo, hi = max(j - 1, 0), min(j + 2, blocks)
        detect[:, j * 128 : (j + 1) * 128] = jnp.dot(
            filtered[:, lo * 128 : hi * 128],
            horiz[(lo - j + 1) * 128 : (hi - j + 1) * 128, :],
            preferred_element_type=F32,
        )


def shards(
    warped_tiles,
    coefficients,
    tile_weight,
    tile_cell,
    tile_valid,
    dest_patch,
    basis_taps,
    filter_taps,
):
    count, size = warped_tiles.shape[:2]
    nb, _, nt = basis_taps.shape
    nf = filter_taps.shape[1]
    patches, V = lax.axis_size("patch"), lax.axis_size("visit")
    X, Y, Z = patches // 2, 2, V // 2
    R = CELL_ROWS * size // V
    crossed = X == Y
    n1, n2 = X, Y
    cfg = (X, Y, Z, R, nb, count, n1, n2)
    patch, visit = lax.axis_index("patch"), lax.axis_index("visit")
    x, core, z, y = patch // 2, patch % 2, visit // Y, visit % Y
    swap = core if crossed else core * 0
    scal = jnp.stack([x, core, z, y, swap]).astype(jnp.int32)

    def send(value, move):
        pairs = []
        for v in range(V):
            for p in range(patches):
                z, y, x, core = move(v // Y, v % Y, p // 2, p % 2)
                pairs.append((v * patches + p, (z * Y + y) * patches + x * 2 + core))
        return lax.ppermute(value, ("visit", "patch"), pairs)

    def to_core(value):
        return send(value, lambda z, y, x, core: (z, y, x, 1 - core))

    def hop(value, k, first):
        def move(z, y, x, core):
            if first != (crossed and core == 1):
                return z, y, (x + k) % X, core
            return z, (y + k) % Y, x, core

        return send(value, move)

    def to_z(value, k):
        return send(value, lambda z, y, x, core: ((z + k) % Z, y, x, core))

    tiles_other = to_core(warped_tiles)
    effective = lax.reduce_precision(
        tile_weight.astype(F32) * tile_valid.astype(F32), exponent_bits=8, mantissa_bits=7
    )
    scales = lax.reduce_precision(
        coefficients.T.astype(F32) * effective[None, :], exponent_bits=8, mantissa_bits=7
    )
    keys = (dest_patch * CELLS + tile_cell).astype(F32)
    info = jnp.concatenate(
        [scales, effective[None], jnp.zeros((5 - nb, count), F32), keys[None], keys[None]], axis=0
    )
    info = jnp.pad(info, ((0, 0), (0, 128 - count)))
    info_other = to_core(info)

    basis = jnp.concatenate([basis_taps[:, 0, :], basis_taps[:, 1, ::-1]], axis=0).astype(F32)
    filt = jnp.concatenate([filter_taps[:1], filter_taps[1:, ::-1]], axis=0).astype(F32)
    basis = jnp.pad(basis, ((0, 0), (0, 128 - nt)))
    filt = jnp.pad(filt, ((0, 0), (0, 128 - nf)))
    fast = crossed
    limit = pltpu.CompilerParams(vmem_limit_bytes=12 << 20) if fast else None

    def array(shape, dtype):
        return pltpu.VMEM(shape, dtype) if fast else jax.ShapeDtypeStruct(shape, dtype)

    def near(value):
        return pltpu.with_memory_space_constraint(value, pltpu.VMEM) if fast else value

    def call(kernel, name, small, arrays, outs, scratch=()):
        return pl.pallas_call(
            kernel,
            out_shape=tuple(array(*out) for out in outs),
            in_specs=[SMEM] * len(small) + [VMEM] * len(arrays),
            out_specs=tuple([VMEM] * len(outs)),
            scratch_shapes=list(scratch),
            compiler_params=limit,
            name=name,
        )(*small, *[near(value) for value in arrays])

    row_cat, col_cat, vert, horiz = call(
        functools.partial(mats_kernel, nb=nb, nt=nt, nf=nf, size=size, strip=R),
        "mats",
        [],
        [basis, filt],
        [
            ((size, nb * size), BF16),
            ((size, nb * size), BF16),
            ((R, R + 2 * EDGE), BF16),
            ((3 * size, 128), BF16),
        ],
    )
    strips = []
    for index, (h0, h1) in enumerate(SETS):
        nh = h1 - h0
        block = Z * nh * R
        weights = ((WKEEP, 128), F32)
        acc, w, *sends = call(
            functools.partial(match_kernel, cfg=cfg, h0=h0, nh=nh),
            f"match{index}",
            [scal],
            [info, info_other, warped_tiles, tiles_other, row_cat, col_cat],
            [((X, Y, Z, nh, R, 128), F32), weights]
            + [((n2 * block + WSEND, 128), BF16)] * (n1 - 1),
            [
                pltpu.SMEM((2 * count + UNROLL,), jnp.int32),
                pltpu.VMEM((2, nb * size, UNROLL * size), BF16),
                pltpu.SMEM((8, 128), F32),
                pltpu.SMEM((8, 128), F32),
                pltpu.SemaphoreType.DMA((2,)),
            ],
        )
        others = [hop(value, k + 1, True) for k, value in enumerate(sends)]
        keep, w, *sends = call(
            functools.partial(first_add_kernel, cfg=cfg, nh=nh),
            f"add1_{index}",
            [scal],
            [acc, w, *others],
            [((Z, nh, R, 128), F32), weights] + [((block + WSEND, 128), BF16)] * (n2 - 1),
        )
        others = [hop(value, k + 1, False) for k, value in enumerate(sends)]
        keep, w, *sends = call(
            functools.partial(second_add_kernel, cfg=cfg, nh=nh),
            f"add2_{index}",
            [scal],
            [keep, w, *others],
            [((nh, R, 128), F32), weights] + [((nh * R + WSEND, 128), BF16)] * (Z - 1),
        )
        others = [to_z(value, k + 1) for k, value in enumerate(sends)]
        last = index == len(SETS) - 1
        strip, *edges = call(
            functools.partial(coadd_kernel, cfg=cfg, h0=h0, nh=nh, last=last),
            f"coadd{index}",
            [scal],
            [keep, w, *others] + (strips if last else []),
            [((R, nh * 128), F32)] + ([((EDGE, CELL_COLS * size), BF16)] * 2 if last else []),
        )
        strips.append(strip)
    top, bottom = edges
    above = lax.ppermute(bottom, "visit", [(i, i + 1) for i in range(V - 1)])
    below = lax.ppermute(top, "visit", [(i + 1, i) for i in range(V - 1)])
    arrays = [vert, horiz, above, below, *strips]
    coadd, detect = pl.pallas_call(
        detect_kernel,
        out_shape=(
            jax.ShapeDtypeStruct((R, CELL_COLS * size), F32),
            jax.ShapeDtypeStruct((R, CELL_COLS * size), F32),
        ),
        in_specs=[VMEM] * len(arrays),
        out_specs=(VMEM, VMEM),
        scratch_shapes=[pltpu.VMEM((R, CELL_COLS * size), BF16)],
        compiler_params=limit,
        name="detect",
    )(*[near(value) for value in arrays])
    return coadd[None], detect[None]


def solution(mesh):
    in_specs = (
        P(("visit", "patch"), None, None),
        P(("visit", "patch"), None),
        P(("visit", "patch")),
        P(("visit", "patch")),
        P(("visit", "patch")),
        P(("visit", "patch")),
        P(),
        P(),
    )
    out_specs = (P("patch", "visit", None), P("patch", "visit", None))
    return jax.shard_map(shards, mesh=mesh, in_specs=in_specs, out_specs=out_specs, check_vma=False)
```

time: 613 us -> 91.1 us (0.15)
  the two profiles are of different devices: /device:TPU:8 before, /device:TPU:0 now
where the time goes in v2:
time: 91.1 us; the launch traced here: 91.2 us
  waiting for transfers between devices  37.6 us (41%)
  starting transfers between devices  27.2 us (30%)
  Pallas kernels  20.1 us (22%)
  local copies, waits for them, and re-layouts  3.36 us (4%)
  other arithmetic  2.07 us (2%)
    ppermute x12, waiting for transfers between devices, send(): return lax.ppermute(value, ('visit', 'patch'), pairs)  29.6 us
    ppermute x12, starting transfers between devices, send(): return lax.ppermute(value, ('visit', 'patch'), pairs)  24.1 us
    pallas_call x9, Pallas kernels, call(): pl.pallas_call(kernel, out_shape=tuple((array(*out) for out in outs)), in...  18.7 us
    ppermute x1, waiting for transfers between devices, shards(): below = lax.ppermute(top, 'visit', [(i + 1, i) for i in range(V - 1)])  7.37 us
  transfers between devices with their start and end apart: 14, of which 8 were waited for; matrix products, arithmetic and copies ran while one was open for 4% of the time, Pallas kernels for 12%

profile of v2, /device:TPU:0, one launch (start us, length us, event | category | flops | bytes accessed | tf_op | source)
XLA Modules:
  0.0 91.2 jit_solution(10556567864714402825)
XLA Ops:
  0.6 0.6 collective-permute-start.1
  1.2 0.7 multiply_reduce-precision_fusion
  1.9 0.7 convert_bitcast_fusion
  2.5 0.7 reduce-precision_bitcast_fusion
  3.2 0.1 collective-permute-start
  3.3 0.7 fusion.9
  4.1 0.1 rev.7
  4.2 0.8 fusion.8
  4.9 0.1 rev.6
  5.1 0.4 mats.1
  5.5 0.1 stack.20.scal
  5.6 0.0 collective-permute-done.info_other
  5.6 0.0 collective-permute-done.1.tiles_other
  5.6 0.0 copy-start
  5.6 1.6 %copy-done = bf16[64,128,128]{2,1,0:T(8,128)(2,1)S(1)} copy-done((bf16[64,128,128]{2,1,0:T(8,128)(2,1)S(1)}, bf16[64,128,128]{2,1,0:T(8,128)(2,1)}, u32[]{:S(2)}) %copy-start) | copy-done | bytes 2097176
  7.2 7.0 %match0.1 = (f32[2,2,4,4,128,128]{5,4,3,2,1,0:T(8,128)S(1)}, f32[8,128]{1,0:T(8,128)S(1)}, bf16[4128,128]{1,0:T(8,128)(2,1)S(1)}) custom-call(s32[5]{0:T(128)S(1)} %stack.20.scal, f32[8,128]{1,0:T(8,128)S(1)} %select_maximum_fusion.info_own, f32[8,128]{1,0:T(8,128)S(1)} %collective-permute-done.info_other, bf16[64,128,128]{2,1,0:T(8,128)(2,1)S(1)} %copy-done, ...), custom_call_target="tpu_custom_call" | custom-call | tf_op jit(solution)/shard_map/match0/pallas_call | solution.py:343
  14.3 3.0 %collective-permute-start.7 = (bf16[4128,128]{1,0:T(8,128)(2,1)S(1)}, bf16[4128,128]{1,0:T(8,128)(2,1)S(1)}, u32[]{:S(2)}, u32[]{:S(2)}) collective-permute-start(bf16[4128,128]{1,0:T(8,128)(2,1)S(1)} %get-tuple-element.50), channel_id=1, source_target_pairs={{0,2},{1,5},{2,0},{3,7},{4,6},{5,1},{6,4},{7,3},{8,10},{9,13},{10,... | collective-permute-start | bytes 3170312 | tf_op jit(solution)/shard_map/ppermute | solution.py:299
  17.3 6.9 %match1.1 = (f32[2,2,4,4,128,128]{5,4,3,2,1,0:T(8,128)S(1)}, f32[8,128]{1,0:T(8,128)S(1)}, bf16[4128,128]{1,0:T(8,128)(2,1)S(1)}) custom-call(s32[5]{0:T(128)S(1)} %stack.20.scal, f32[8,128]{1,0:T(8,128)S(1)} %select_maximum_fusion.info_own, f32[8,128]{1,0:T(8,128)S(1)} %collective-permute-done.info_other, bf16[64,128,128]{2,1,0:T(8,128)(2,1)S(1)} %copy-done, ...), custom_call_target="tpu_custom_call" | custom-call | tf_op jit(solution)/shard_map/match1/pallas_call | solution.py:343
  24.2 1.3 %collective-permute-start.2 = (bf16[4128,128]{1,0:T(8,128)(2,1)S(1)}, bf16[4128,128]{1,0:T(8,128)(2,1)S(1)}, u32[]{:S(2)}, u32[]{:S(2)}) collective-permute-start(bf16[4128,128]{1,0:T(8,128)(2,1)S(1)} %get-tuple-element.39), channel_id=1, source_target_pairs={{0,2},{1,5},{2,0},{3,7},{4,6},{5,1},{6,4},{7,3},{8,10},{9,13},{10,... | collective-permute-start | bytes 3170312 | tf_op jit(solution)/shard_map/ppermute | solution.py:299
  25.5 4.7 %collective-permute-done.7.refs_0_ = bf16[4128,128]{1,0:T(8,128)(2,1)S(1)} collective-permute-done((bf16[4128,128]{1,0:T(8,128)(2,1)S(1)}, bf16[4128,128]{1,0:T(8,128)(2,1)S(1)}, u32[]{:S(2)}, u32[]{:S(2)}) %collective-permute-start.7) | collective-permute-done | bytes 1056800 | tf_op jit(solution)/shard_map/ppermute | solution.py:299
  30.2 0.8 add1_0.1
  31.0 2.8 %collective-permute-start.8 = (bf16[2080,128]{1,0:T(8,128)(2,1)S(1)}, bf16[2080,128]{1,0:T(8,128)(2,1)S(1)}, u32[]{:S(2)}, u32[]{:S(2)}) collective-permute-start(bf16[2080,128]{1,0:T(8,128)(2,1)S(1)} %get-tuple-element.53), channel_id=1, source_target_pairs={{0,4},{1,3},{2,6},{3,1},{4,0},{5,7},{6,2},{7,5},{8,12},{9,11},{10,... | collective-permute-start | bytes 1597448 | tf_op jit(solution)/shard_map/ppermute | solution.py:299
  33.7 12.5 %collective-permute-done.2.refs_0_ = bf16[4128,128]{1,0:T(8,128)(2,1)S(1)} collective-permute-done((bf16[4128,128]{1,0:T(8,128)(2,1)S(1)}, bf16[4128,128]{1,0:T(8,128)(2,1)S(1)}, u32[]{:S(2)}, u32[]{:S(2)}) %collective-permute-start.2) | collective-permute-done | bytes 1056800 | tf_op jit(solution)/shard_map/ppermute | solution.py:299
  46.3 0.8 add1_1.1
  47.1 3.7 %collective-permute-start.3 = (bf16[2080,128]{1,0:T(8,128)(2,1)S(1)}, bf16[2080,128]{1,0:T(8,128)(2,1)S(1)}, u32[]{:S(2)}, u32[]{:S(2)}) collective-permute-start(bf16[2080,128]{1,0:T(8,128)(2,1)S(1)} %get-tuple-element.42), channel_id=1, source_target_pairs={{0,4},{1,3},{2,6},{3,1},{4,0},{5,7},{6,2},{7,5},{8,12},{9,11},{10,... | collective-permute-start | bytes 1597448 | tf_op jit(solution)/shard_map/ppermute | solution.py:299
  50.8 0.0 collective-permute-done.8.refs_0_
  50.8 0.6 add2_0.1
  51.4 0.1 collective-permute-start.9
  51.5 4.7 %collective-permute-start.10 = (bf16[544,128]{1,0:T(8,128)(2,1)S(1)}, bf16[544,128]{1,0:T(8,128)(2,1)S(1)}, u32[]{:S(2)}, u32[]{:S(2)}) collective-permute-start(bf16[544,128]{1,0:T(8,128)(2,1)S(1)} %get-tuple-element.57), channel_id=1, source_target_pairs={{0,16},{1,17},{2,18},{3,19},{4,20},{5,21},{6,22},{7,23},{8,24},{9,... | collective-permute-start | bytes 417800 | tf_op jit(solution)/shard_map/ppermute | solution.py:299
  56.2 1.3 %collective-permute-start.11 = (bf16[544,128]{1,0:T(8,128)(2,1)S(1)}, bf16[544,128]{1,0:T(8,128)(2,1)S(1)}, u32[]{:S(2)}, u32[]{:S(2)}) collective-permute-start(bf16[544,128]{1,0:T(8,128)(2,1)S(1)} %get-tuple-element.58), channel_id=1, source_target_pairs={{0,24},{1,25},{2,26},{3,27},{4,28},{5,29},{6,30},{7,31},{8,0},{9,1... | collective-permute-start | bytes 417800 | tf_op jit(solution)/shard_map/ppermute | solution.py:299
  57.5 0.5 collective-permute-done.3.refs_0_
  58.0 0.7 add2_1.1
  58.7 2.1 %collective-permute-start.4 = (bf16[544,128]{1,0:T(8,128)(2,1)S(1)}, bf16[544,128]{1,0:T(8,128)(2,1)S(1)}, u32[]{:S(2)}, u32[]{:S(2)}) collective-permute-start(bf16[544,128]{1,0:T(8,128)(2,1)S(1)} %get-tuple-element.45), channel_id=1, source_target_pairs={{0,8},{1,9},{2,10},{3,11},{4,12},{5,13},{6,14},{7,15},{8,16},{9,17... | collective-permute-start | bytes 417800 | tf_op jit(solution)/shard_map/ppermute | solution.py:299
  60.8 2.6 %collective-permute-start.5 = (bf16[544,128]{1,0:T(8,128)(2,1)S(1)}, bf16[544,128]{1,0:T(8,128)(2,1)S(1)}, u32[]{:S(2)}, u32[]{:S(2)}) collective-permute-start(bf16[544,128]{1,0:T(8,128)(2,1)S(1)} %get-tuple-element.46), channel_id=1, source_target_pairs={{0,16},{1,17},{2,18},{3,19},{4,20},{5,21},{6,22},{7,23},{8,24},{9,... | collective-permute-start | bytes 417800 | tf_op jit(solution)/shard_map/ppermute | solution.py:299
  63.5 0.0 collective-permute-done.9.refs_0_
  63.5 1.9 %collective-permute-start.6 = (bf16[544,128]{1,0:T(8,128)(2,1)S(1)}, bf16[544,128]{1,0:T(8,128)(2,1)S(1)}, u32[]{:S(2)}, u32[]{:S(2)}) collective-permute-start(bf16[544,128]{1,0:T(8,128)(2,1)S(1)} %get-tuple-element.47), channel_id=1, source_target_pairs={{0,24},{1,25},{2,26},{3,27},{4,28},{5,29},{6,30},{7,31},{8,0},{9,1... | collective-permute-start | bytes 417800 | tf_op jit(solution)/shard_map/ppermute | solution.py:299
  65.3 1.2 %collective-permute-done.10.refs_1_ = bf16[544,128]{1,0:T(8,128)(2,1)S(1)} collective-permute-done((bf16[544,128]{1,0:T(8,128)(2,1)S(1)}, bf16[544,128]{1,0:T(8,128)(2,1)S(1)}, u32[]{:S(2)}, u32[]{:S(2)}) %collective-permute-start.10) | collective-permute-done | bytes 139296 | tf_op jit(solution)/shard_map/ppermute | solution.py:299
  66.6 0.0 collective-permute-done.11.refs_2_
  66.6 0.7 coadd0.1.refs_3_.refs_0_
  67.3 1.4 %collective-permute-done.4.refs_0_ = bf16[544,128]{1,0:T(8,128)(2,1)S(1)} collective-permute-done((bf16[544,128]{1,0:T(8,128)(2,1)S(1)}, bf16[544,128]{1,0:T(8,128)(2,1)S(1)}, u32[]{:S(2)}, u32[]{:S(2)}) %collective-permute-start.4) | collective-permute-done | bytes 139296 | tf_op jit(solution)/shard_map/ppermute | solution.py:299
  68.6 9.3 %collective-permute-done.5.refs_1_ = bf16[544,128]{1,0:T(8,128)(2,1)S(1)} collective-permute-done((bf16[544,128]{1,0:T(8,128)(2,1)S(1)}, bf16[544,128]{1,0:T(8,128)(2,1)S(1)}, u32[]{:S(2)}, u32[]{:S(2)}) %collective-permute-start.5) | collective-permute-done | bytes 139296 | tf_op jit(solution)/shard_map/ppermute | solution.py:299
  77.9 0.0 collective-permute-done.6.refs_2_
  77.9 0.7 coadd1.1
  78.7 1.8 %collective-permute-start.12 = (bf16[32,1024]{1,0:T(8,128)(2,1)S(1)}, bf16[32,1024]{1,0:T(8,128)(2,1)S(1)}, u32[]{:S(2)}, u32[]{:S(2)}) collective-permute-start(bf16[32,1024]{1,0:T(8,128)(2,1)S(1)} %get-tuple-element.59), channel_id=1, source_target_pairs={{0,4},{4,8},{8,12},{12,16},{16,20},{20,24},{24,28},{1,5},{5,9},{9,... | collective-permute-start | bytes 196616 | tf_op jit(solution)/shard_map/ppermute | solution.py:412
  80.5 1.3 %collective-permute-start.13 = (bf16[32,1024]{1,0:T(8,128)(2,1)S(1)}, bf16[32,1024]{1,0:T(8,128)(2,1)S(1)}, u32[]{:S(2)}, u32[]{:S(2)}) collective-permute-start(bf16[32,1024]{1,0:T(8,128)(2,1)S(1)} %get-tuple-element.60), channel_id=1, source_target_pairs={{4,0},{8,4},{12,8},{16,12},{20,16},{24,20},{28,24},{5,1},{9,5},{13... | collective-permute-start | bytes 196616 | tf_op jit(solution)/shard_map/ppermute | solution.py:413
  81.8 0.6 collective-permute-done.12.above
  82.3 7.4 %collective-permute-done.13.below = bf16[32,1024]{1,0:T(8,128)(2,1)S(1)} collective-permute-done((bf16[32,1024]{1,0:T(8,128)(2,1)S(1)}, bf16[32,1024]{1,0:T(8,128)(2,1)S(1)}, u32[]{:S(2)}, u32[]{:S(2)}) %collective-permute-start.13) | collective-permute-done | bytes 65568 | tf_op jit(solution)/shard_map/ppermute | solution.py:413
  89.7 1.4 %detect.1 = (f32[128,1024]{1,0:T(8,128)}, f32[128,1024]{1,0:T(8,128)}) custom-call(bf16[128,192]{1,0:T(8,128)(2,1)S(1)} %get-tuple-element.33.vert, bf16[384,128]{1,0:T(8,128)(2,1)S(1)} %get-tuple-element.34.horiz, bf16[32,1024]{1,0:T(8,128)(2,1)S(1)} %collective-permute-done.12.above, bf16[32,1024]{1,0:T(8,128)(2,1)S(1)} %collective-permute-done.13.below, ...), custom_call_target="tpu_custom_call" | custom-call | tf_op jit(solution)/shard_map/detect/pallas_call | solution.py:415
  (5 shorter events, 0.0 us)
Async XLA Ops:
  0.6 5.0 %collective-permute-start.1 = (bf16[64,128,128]{2,1,0:T(8,128)(2,1)}, bf16[64,128,128]{2,1,0:T(8,128)(2,1)S(1)}, u32[]{:S(2)}, u32[]{:S(2)}) collective-permute-start(bf16[64,128,128]{2,1,0:T(8,128)(2,1)} %tiles_own.3), channel_id=1, source_target_pairs={{0,1},{1,0},{2,3},{3,2},{4,5},{5,4},{6,7},{7,6},{8,9},{9,8},{10,11... | collective-permute-start | bytes 6291464 | tf_op jit(solution)/shard_map/ppermute | solution.py:299
  3.2 2.4 %collective-permute-start = (f32[8,128]{1,0:T(8,128)S(1)}, f32[8,128]{1,0:T(8,128)S(1)}, u32[]{:S(2)}, u32[]{:S(2)}) collective-permute-start(f32[8,128]{1,0:T(8,128)S(1)} %select_maximum_fusion.info_own), channel_id=1, source_target_pairs={{0,1},{1,0},{2,3},{3,2},{4,5},{5,4},{6,7},{7,6},{8,9},{9,8},{10,11... | collective-permute-start | bytes 12296 | tf_op jit(solution)/shard_map/ppermute | solution.py:299
  5.6 1.6 %copy-start = (bf16[64,128,128]{2,1,0:T(8,128)(2,1)S(1)}, bf16[64,128,128]{2,1,0:T(8,128)(2,1)}, u32[]{:S(2)}) copy-start(bf16[64,128,128]{2,1,0:T(8,128)(2,1)} %tiles_own.3) | copy-start | bytes 6291460
  14.3 15.9 %collective-permute-start.7 = (bf16[4128,128]{1,0:T(8,128)(2,1)S(1)}, bf16[4128,128]{1,0:T(8,128)(2,1)S(1)}, u32[]{:S(2)}, u32[]{:S(2)}) collective-permute-start(bf16[4128,128]{1,0:T(8,128)(2,1)S(1)} %get-tuple-element.50), channel_id=1, source_target_pairs={{0,2},{1,5},{2,0},{3,7},{4,6},{5,1},{6,4},{7,3},{8,10},{9,13},{10,... | collective-permute-start | bytes 3170312 | tf_op jit(solution)/shard_map/ppermute | solution.py:299
  24.2 22.0 %collective-permute-start.2 = (bf16[4128,128]{1,0:T(8,128)(2,1)S(1)}, bf16[4128,128]{1,0:T(8,128)(2,1)S(1)}, u32[]{:S(2)}, u32[]{:S(2)}) collective-permute-start(bf16[4128,128]{1,0:T(8,128)(2,1)S(1)} %get-tuple-element.39), channel_id=1, source_target_pairs={{0,2},{1,5},{2,0},{3,7},{4,6},{5,1},{6,4},{7,3},{8,10},{9,13},{10,... | collective-permute-start | bytes 3170312 | tf_op jit(solution)/shard_map/ppermute | solution.py:299
  31.0 19.8 %collective-permute-start.8 = (bf16[2080,128]{1,0:T(8,128)(2,1)S(1)}, bf16[2080,128]{1,0:T(8,128)(2,1)S(1)}, u32[]{:S(2)}, u32[]{:S(2)}) collective-permute-start(bf16[2080,128]{1,0:T(8,128)(2,1)S(1)} %get-tuple-element.53), channel_id=1, source_target_pairs={{0,4},{1,3},{2,6},{3,1},{4,0},{5,7},{6,2},{7,5},{8,12},{9,11},{10,... | collective-permute-start | bytes 1597448 | tf_op jit(solution)/shard_map/ppermute | solution.py:299
  47.1 11.0 %collective-permute-start.3 = (bf16[2080,128]{1,0:T(8,128)(2,1)S(1)}, bf16[2080,128]{1,0:T(8,128)(2,1)S(1)}, u32[]{:S(2)}, u32[]{:S(2)}) collective-permute-start(bf16[2080,128]{1,0:T(8,128)(2,1)S(1)} %get-tuple-element.42), channel_id=1, source_target_pairs={{0,4},{1,3},{2,6},{3,1},{4,0},{5,7},{6,2},{7,5},{8,12},{9,11},{10,... | collective-permute-start | bytes 1597448 | tf_op jit(solution)/shard_map/ppermute | solution.py:299
  51.4 12.0 %collective-permute-start.9 = (bf16[544,128]{1,0:T(8,128)(2,1)S(1)}, bf16[544,128]{1,0:T(8,128)(2,1)S(1)}, u32[]{:S(2)}, u32[]{:S(2)}) collective-permute-start(bf16[544,128]{1,0:T(8,128)(2,1)S(1)} %get-tuple-element.56), channel_id=1, source_target_pairs={{0,8},{1,9},{2,10},{3,11},{4,12},{5,13},{6,14},{7,15},{8,16},{9,17... | collective-permute-start | bytes 417800 | tf_op jit(solution)/shard_map/ppermute | solution.py:299
  51.5 15.1 %collective-permute-start.10 = (bf16[544,128]{1,0:T(8,128)(2,1)S(1)}, bf16[544,128]{1,0:T(8,128)(2,1)S(1)}, u32[]{:S(2)}, u32[]{:S(2)}) collective-permute-start(bf16[544,128]{1,0:T(8,128)(2,1)S(1)} %get-tuple-element.57), channel_id=1, source_target_pairs={{0,16},{1,17},{2,18},{3,19},{4,20},{5,21},{6,22},{7,23},{8,24},{9,... | collective-permute-start | bytes 417800 | tf_op jit(solution)/shard_map/ppermute | solution.py:299
  56.2 10.4 %collective-permute-start.11 = (bf16[544,128]{1,0:T(8,128)(2,1)S(1)}, bf16[544,128]{1,0:T(8,128)(2,1)S(1)}, u32[]{:S(2)}, u32[]{:S(2)}) collective-permute-start(bf16[544,128]{1,0:T(8,128)(2,1)S(1)} %get-tuple-element.58), channel_id=1, source_target_pairs={{0,24},{1,25},{2,26},{3,27},{4,28},{5,29},{6,30},{7,31},{8,0},{9,1... | collective-permute-start | bytes 417800 | tf_op jit(solution)/shard_map/ppermute | solution.py:299
  58.7 9.9 %collective-permute-start.4 = (bf16[544,128]{1,0:T(8,128)(2,1)S(1)}, bf16[544,128]{1,0:T(8,128)(2,1)S(1)}, u32[]{:S(2)}, u32[]{:S(2)}) collective-permute-start(bf16[544,128]{1,0:T(8,128)(2,1)S(1)} %get-tuple-element.45), channel_id=1, source_target_pairs={{0,8},{1,9},{2,10},{3,11},{4,12},{5,13},{6,14},{7,15},{8,16},{9,17... | collective-permute-start | bytes 417800 | tf_op jit(solution)/shard_map/ppermute | solution.py:299
  60.8 17.1 %collective-permute-start.5 = (bf16[544,128]{1,0:T(8,128)(2,1)S(1)}, bf16[544,128]{1,0:T(8,128)(2,1)S(1)}, u32[]{:S(2)}, u32[]{:S(2)}) collective-permute-start(bf16[544,128]{1,0:T(8,128)(2,1)S(1)} %get-tuple-element.46), channel_id=1, source_target_pairs={{0,16},{1,17},{2,18},{3,19},{4,20},{5,21},{6,22},{7,23},{8,24},{9,... | collective-permute-start | bytes 417800 | tf_op jit(solution)/shard_map/ppermute | solution.py:299
  63.5 14.5 %collective-permute-start.6 = (bf16[544,128]{1,0:T(8,128)(2,1)S(1)}, bf16[544,128]{1,0:T(8,128)(2,1)S(1)}, u32[]{:S(2)}, u32[]{:S(2)}) collective-permute-start(bf16[544,128]{1,0:T(8,128)(2,1)S(1)} %get-tuple-element.47), channel_id=1, source_target_pairs={{0,24},{1,25},{2,26},{3,27},{4,28},{5,29},{6,30},{7,31},{8,0},{9,1... | collective-permute-start | bytes 417800 | tf_op jit(solution)/shard_map/ppermute | solution.py:299
  78.7 3.7 %collective-permute-start.12 = (bf16[32,1024]{1,0:T(8,128)(2,1)S(1)}, bf16[32,1024]{1,0:T(8,128)(2,1)S(1)}, u32[]{:S(2)}, u32[]{:S(2)}) collective-permute-start(bf16[32,1024]{1,0:T(8,128)(2,1)S(1)} %get-tuple-element.59), channel_id=1, source_target_pairs={{0,4},{4,8},{8,12},{12,16},{16,20},{20,24},{24,28},{1,5},{5,9},{9,... | collective-permute-start | bytes 196616 | tf_op jit(solution)/shard_map/ppermute | solution.py:412
  80.5 9.3 %collective-permute-start.13 = (bf16[32,1024]{1,0:T(8,128)(2,1)S(1)}, bf16[32,1024]{1,0:T(8,128)(2,1)S(1)}, u32[]{:S(2)}, u32[]{:S(2)}) collective-permute-start(bf16[32,1024]{1,0:T(8,128)(2,1)S(1)} %get-tuple-element.60), channel_id=1, source_target_pairs={{4,0},{8,4},{12,8},{16,12},{20,16},{24,20},{28,24},{5,1},{9,5},{13... | collective-permute-start | bytes 196616 | tf_op jit(solution)/shard_map/ppermute | solution.py:413
